TPU v7x, 512 devices: a whole 4x8x8 slice. The times are simulated.
512 devices in a mesh: rep: 16 (over z, core), tp: 32 (over y, x).
Axes of the slice: x: 4, y: 8, z: 8, core: 2. Of those that a mesh axis runs over, the one named last changes fastest.
Arguments:
- attn: bfloat16 [12288, 4096], P('rep', 'tp'), parts along dimension 0, may hold values from -6 to 6
- output_weight: bfloat16 [4096, 8192], P(None, 'tp'), may hold values from -0.09375 to 0.09375
- adapter_down_weight: bfloat16 [32, 64, 4096], P('tp'), may hold values from -0.09375 to 0.09375
- adapter_up_weight: bfloat16 [32, 64, 8192], P('tp'), may hold values from -0.75 to 0.75
- block_adapter_index: int32 [96], P('rep'), parts along dimension 0, may hold values from 0 to 31
- adapter_page_table: int32 [32], replicated, may hold values from 0 to 31, each once
Outputs:
- projected: bfloat16 [12288, 8192], P('rep', 'tp'), parts along dimension 0
There are 16 independent parts, one for each index of `rep`. A program takes and returns all parts, laid end to end along the dimension named above; an argument that names none is the same for every part. Nothing has to cross between parts.
Inputs may be any that keep to these rules, and one draw needn't show every extreme that they name: adapter_page_table is a permutation; adapter a is stored on tp device adapter_page_table[a] (each device holds exactly one adapter), and row adapter_page_table[a] of adapter_down_weight and adapter_up_weight holds it. `block_adapter_index`: the adapter used by all 128 tokens of a block.
All inputs are finite; a program needn't handle non-finite values.
Results may differ from a plain program's by a relative error of at most 0.0046.
Values may be sent and summed in bfloat16 or wider, within the bound.
No kernel may reach another device: no remote copies, remote signals or barrier semaphores. Data moves between devices by JAX's collectives and lax.ppermute only.
A program may use at most 64 MiB of HBM per device.

v0:
```python
import jax
import jax.numpy as jnp
from jax import lax

MODEL_WIDTH = 8192
BLOCK = 128
TOKENS = 768
ATTN_FEATURES = 4096
BLOCKS = 6


adapter_scale = 2.0


def reference(
    attn,
    output_weight,
    adapter_down_weight,
    adapter_up_weight,
    block_adapter_index,
    adapter_page_table,
):
    block_page_index = adapter_page_table[block_adapter_index].astype(jnp.int32)
    base_output = jnp.dot(attn, output_weight, preferred_element_type=jnp.float32)
    row_blocks = attn.reshape(BLOCKS, BLOCK, ATTN_FEATURES).astype(jnp.float32)
    down_block_rows = adapter_down_weight[block_page_index].astype(jnp.float32)
    shrunk = jnp.einsum(
        "btf,brf->brt", row_blocks, down_block_rows, precision=lax.Precision.HIGHEST
    )
    shrunk_low = lax.optimization_barrier(shrunk.astype(jnp.bfloat16))
    up_block_rows = adapter_up_weight[block_page_index].astype(jnp.float32)
    adapter_output = jnp.einsum(
        "brt,brc->btc",
        shrunk_low.astype(jnp.float32),
        up_block_rows,
        precision=lax.Precision.HIGHEST,
    )
    adapter_output = adapter_output.reshape(TOKENS, MODEL_WIDTH)
    return (base_output + adapter_scale * adapter_output).astype(jnp.bfloat16)


def apart(x, dim, parts):
    return x.reshape(x.shape[:dim] + (parts, x.shape[dim] // parts) + x.shape[dim + 1 :])


def together(x, dim):
    return x.reshape(x.shape[:dim] + (x.shape[dim] * x.shape[dim + 1],) + x.shape[dim + 2 :])


def solution(mesh):
    parts = mesh.shape["rep"]

    def whole(*arrays):
        each = [
            a if d is None else apart(a, d, parts)
            for a, d in zip(arrays, (0, None, None, None, 0, None))
        ]
        made = jax.vmap(reference, in_axes=(0, None, None, None, 0, None), out_axes=0)(*each)
        return together(made, 0)

    return whole
```

profile of v0, /device:TPU:64, one launch (start us, length us, event | category | flops | bytes accessed | tf_op | source)
XLA Modules:
  0.0 219.7 jit_solution(1711944200849320129)
XLA Ops:
  6.5 0.0 copy-start
  6.5 0.0 copy-start.2
  6.5 0.0 copy-start.4
  6.5 0.0 all-gather.5.cloned.1.call-start
  6.6 0.7 all-gather.5.cloned.1.call-update
  7.3 2.0 copy_bitcast_fusion.1
  9.3 9.9 %all-to-all-start = ((bf16[1,64,32,128]{3,1,0,2:T(8,128)(2,1)}), bf16[1,64,32,128]{3,1,0,2:T(8,128)(2,1)S(1)}, u32[]{:S(2)}, u32[]{:S(2)}) async-start(bf16[1,64,32,128]{3,1,0,2:T(8,128)(2,1)} %copy_bitcast_fusion.1), calls=%async_computation | async-start | bytes 1048576 | tf_op jit(solution)/call_exported
  19.2 2.3 %copy.10 = bf16[1,8,32,8,256]{4,3,1,0,2:T(8,128)(2,1)} copy(bf16[1,8,32,8,256]{4,3,2,1,0:T(8,128)(2,1)} %bitcast.50) | data formatting | bytes 2097152 | tf_op jit(solution)/call_exported
  21.6 15.4 %all-to-all-done = bf16[1,64,32,128]{3,1,0,2:T(8,128)(2,1)S(1)} async-done(((bf16[1,64,32,128]{3,1,0,2:T(8,128)(2,1)}), bf16[1,64,32,128]{3,1,0,2:T(8,128)(2,1)S(1)}, u32[]{:S(2)}, u32[]{:S(2)}) %all-to-all-start) | async-done | bytes 524320 | tf_op jit(solution)/call_exported
  37.0 0.8 copy-done.3
  37.7 4.7 %all-to-all-start.1 = ((bf16[1,64,32,256]{3,1,0,2:T(8,128)(2,1)}), bf16[1,64,32,256]{3,1,0,2:T(8,128)(2,1)S(1)}, u32[]{:S(2)}, u32[]{:S(2)}) async-start(bf16[1,64,32,256]{3,1,0,2:T(8,128)(2,1)} %bitcast.48), calls=%async_computation.1 | async-start | bytes 2097152 | tf_op jit(solution)/call_exported
  42.4 0.0 copy-done.4
  42.5 0.0 copy-done.1
  42.5 0.6 gather_fusion
  43.1 2.2 %gather_fusion.1 = bf16[6,64,128]{2,1,0:T(8,128)(2,1)} fusion(bf16[32,64,128]{2,1,0:T(8,128)(2,1)} %bitcast.53, s32[1024]{0:T(1024)S(1)} %pad_clamp_fusion), kind=kCustom, calls=%fused_computation.1 | custom fusion | bytes 196632 | tf_op jit(solution)/vmap()/gather | solution.py:26
  45.4 0.0 copy-done.2
  45.4 1.1 convolution_bitcast_fusion.1
  46.5 159.2 %all-reduce.2 = bf16[1,6,64,128]{3,2,1,0:T(8,128)(2,1)} all-reduce(f32[1,6,64,128]{3,2,1,0:T(8,128)S(1)} %convolution_bitcast_fusion.1), channel_id=4, replica_groups=[16,32]<=[512], use_global_device_ids=true, to_apply=%add.clone | all-reduce | flops 49152 | bytes 294912 | tf_op jit(solution)/vmap(btf,brf->brt)/dot_general | solution.py:27
  205.7 0.0 all-to-all-done.1
  205.7 0.6 gather_fusion.2
  206.3 1.2 convolution_multiply_fusion
  207.5 0.0 all-gather.5.cloned.1.call-done
  207.5 0.0 copy-done
  207.5 5.3 %fusion.2 = bf16[768,256]{1,0:T(8,128)(2,1)} fusion(f32[1,768,256]{2,1,0:T(8,128)S(1)} %bitcast.51, bf16[768,4096]{1,0:T(8,128)(2,1)} %all-gather.5.cloned.1.call-done, bf16[4096,256]{1,0:T(8,128)(2,1)S(1)} %copy-done), kind=kOutput, calls=%fused_computation.7 | convolution fusion | flops 1611005952 | bytes 9568256 | tf_op jit(solution)/vmap()/dot_general | solution.py:24
  (6 shorter events, 0.0 us)
Async XLA Ops:
  6.5 201.0 %copy-start = (bf16[4096,256]{1,0:T(8,128)(2,1)S(1)}, bf16[4096,256]{1,0:T(8,128)(2,1)}, u32[]{:S(2)}) copy-start(bf16[4096,256]{1,0:T(8,128)(2,1)} %param.1) | copy-start | bytes 6291460
  6.5 38.8 %copy-start.2 = (bf16[768,128]{1,0:T(8,128)(2,1)S(1)}, bf16[768,128]{1,0:T(8,128)(2,1)}, u32[]{:S(2)}) copy-start(bf16[768,128]{1,0:T(8,128)(2,1)} %param) | copy-start | bytes 589828
  6.5 35.9 %copy-start.4 = (s32[6]{0:T(128)S(1)}, s32[6]{0:T(128)}, u32[]{:S(2)}) copy-start(s32[6]{0:T(128)} %param.4) | copy-start | bytes 76
  6.5 35.9 %copy-start.1 = (s32[32]{0:T(128)S(1)}, s32[32]{0:T(128)}, u32[]{:S(2)}) copy-start(s32[32]{0:T(128)} %param.3) | copy-start | bytes 388
  6.5 200.9 %all-gather.5.cloned.1.call-start = ((), (), s32[]{:S(2)}) async-start(), calls=%async_computation.2 | async-start | bytes 6488064 | tf_op jit(solution)/reshape | solution.py:43
  9.3 27.7 %all-to-all-start = ((bf16[1,64,32,128]{3,1,0,2:T(8,128)(2,1)}), bf16[1,64,32,128]{3,1,0,2:T(8,128)(2,1)S(1)}, u32[]{:S(2)}, u32[]{:S(2)}) async-start(bf16[1,64,32,128]{3,1,0,2:T(8,128)(2,1)} %copy_bitcast_fusion.1), calls=%async_computation | async-start | bytes 1048576 | tf_op jit(solution)/call_exported
  37.0 0.8 copy-start.3
  37.7 167.9 %all-to-all-start.1 = ((bf16[1,64,32,256]{3,1,0,2:T(8,128)(2,1)}), bf16[1,64,32,256]{3,1,0,2:T(8,128)(2,1)S(1)}, u32[]{:S(2)}, u32[]{:S(2)}) async-start(bf16[1,64,32,256]{3,1,0,2:T(8,128)(2,1)} %bitcast.48), calls=%async_computation.1 | async-start | bytes 2097152 | tf_op jit(solution)/call_exported
Sparse Core Ops, SparseCore 0:
  10.4 115.7 all-gather.4
where the time goes:
time: 220 us
  blocking collectives  159 us (72%)
  waiting for transfers between devices  16.1 us (7%)
  starting transfers between devices  14.7 us (7%)
  between operations  13.5 us (6%)
  local copies, waits for them, and re-layouts  8.59 us (4%)
  matrix products  7.64 us (3%)
    dot_general x1, blocking collectives, reference(): jnp.einsum('btf,brf->brt', row_blocks, down_block_rows, precision=lax.Pre...  159 us
    another operation x2, waiting for transfers between devices  15.4 us
    another operation x2, starting transfers between devices  14.6 us
    dot_general x1, matrix products, reference(): jnp.dot(attn, output_weight, preferred_element_type=jnp.float32)  5.33 us
  transfers between devices with their start and end apart: 3, of which 1 were waited for; matrix products, arithmetic and copies ran while one was open for 5% of the time, Pallas kernels for 0%

commit v1 on v0

v1 whole, which is shorter than its diff:
```python
import functools

import jax
import jax.numpy as jnp
from jax import lax
from jax.experimental import pallas as pl
from jax.experimental.pallas import tpu as pltpu
from jax.sharding import Mesh, PartitionSpec as P

RANK = 64
BLOCK = 128
NY, PARITIES = 8, 2
CORES = 2
PIECE = 16
adapter_scale = 2.0
MIB = 1 << 20

VMEM = pl.BlockSpec(memory_space=pltpu.VMEM)
SMEM = pl.BlockSpec(memory_space=pltpu.SMEM)
ANY = pl.BlockSpec(memory_space=pl.ANY)


def cost(nbytes, flops=0):
    return pl.CostEstimate(flops=flops, transcendentals=0, bytes_accessed=nbytes)


def params(mib):
    return pltpu.CompilerParams(vmem_limit_bytes=mib * MIB)


def pack_kernel(core_ref, down_ref, up_ref, out_ref, down_half, up_half, sems):
    ranks = down_half.shape[0]
    rows = pl.ds(pl.multiple_of(core_ref[0] * ranks, ranks), ranks)
    copies = [
        pltpu.make_async_copy(down_ref.at[0, rows, :], down_half, sems.at[0]),
        pltpu.make_async_copy(up_ref.at[0, rows, :], up_half, sems.at[1]),
    ]
    for c in copies:
        c.start()
    n = out_ref.shape[0]
    own, width = down_half.shape[1] // n, up_half.shape[1] // n
    copies[0].wait()
    for d in range(n):
        out_ref[d, :, :own] = down_half[:, d * own : (d + 1) * own]
    copies[1].wait()
    for d in range(n):
        out_ref[d, :, own:] = up_half[:, d * width : (d + 1) * width]


def pack(core, down, up, tp):
    ranks = RANK // CORES
    own, width = down.shape[2] // tp, up.shape[2] // tp
    return pl.pallas_call(
        pack_kernel,
        out_shape=jax.ShapeDtypeStruct((tp, ranks, own + width), down.dtype),
        in_specs=[SMEM, ANY, ANY],
        out_specs=VMEM,
        scratch_shapes=[
            pltpu.VMEM((ranks, down.shape[2]), down.dtype),
            pltpu.VMEM((ranks, up.shape[2]), up.dtype),
            pltpu.SemaphoreType.DMA((2,)),
        ],
        compiler_params=params(8),
        cost_estimate=cost(2 * MIB),
    )(core, down, up)


def choose_kernel(index_ref, other_ref, table_ref, pages_ref, own_ref, send_ref, sems):
    n = own_ref.shape[0]
    copies = []
    for b in range(n):
        for i, (who, out) in enumerate(((other_ref, send_ref), (index_ref, own_ref))):
            page = table_ref[who[b]]
            copies.append(pltpu.make_async_copy(pages_ref.at[page], out.at[b], sems.at[i, b]))
    for c in copies:
        c.start()
    for c in copies:
        c.wait()


def choose(index, other, table, pages):
    shape = jax.ShapeDtypeStruct((index.shape[0],) + pages.shape[1:], pages.dtype)
    return pl.pallas_call(
        choose_kernel,
        out_shape=[shape, shape],
        in_specs=[SMEM, SMEM, SMEM, ANY],
        out_specs=[VMEM, VMEM],
        scratch_shapes=[pltpu.SemaphoreType.DMA((2, index.shape[0]))],
        compiler_params=params(8),
        cost_estimate=cost(MIB // 2),
    )(index, other, table, pages)


def shrink_kernel(attn_ref, mine_ref, other_ref, out_ref):
    own = attn_ref.shape[1]
    blocks = mine_ref.shape[0]
    each = RANK // PIECE
    for b in range(blocks):
        down = jnp.concatenate([mine_ref[b, :, :own], other_ref[b, :, :own]], axis=0)
        shrunk = lax.dot_general(
            down,
            attn_ref[b * BLOCK : (b + 1) * BLOCK, :],
            (((1,), (1,)), ((), ())),
            preferred_element_type=jnp.float32,
        ).astype(out_ref.dtype)
        out_ref[b * each : (b + 1) * each] = shrunk.reshape(each, PIECE, BLOCK)
    rest = out_ref.shape[0] - blocks * each
    if rest:
        out_ref[blocks * each :] = jnp.zeros((rest, PIECE, BLOCK), out_ref.dtype)


def shrink(attn, mine, other, tp):
    return pl.pallas_call(
        shrink_kernel,
        out_shape=jax.ShapeDtypeStruct((tp, PIECE, BLOCK), jnp.bfloat16),
        in_specs=[VMEM] * 3,
        out_specs=VMEM,
        compiler_params=params(8),
        cost_estimate=cost(MIB // 2, 2 * attn.size * RANK),
    )(attn, mine, other)


def total_kernel(in_ref, out_ref):
    total = jnp.sum(in_ref[...].astype(jnp.float32), axis=0)
    out_ref[...] = jnp.broadcast_to(total.astype(out_ref.dtype)[None], out_ref.shape)


def total(pieces):
    return pl.pallas_call(
        total_kernel,
        out_shape=jax.ShapeDtypeStruct(pieces.shape, pieces.dtype),
        in_specs=[VMEM],
        out_specs=VMEM,
        compiler_params=params(4),
        cost_estimate=cost(MIB // 4),
    )(pieces)


def matmul_kernel(at_ref, same, low, high, weight, w1, w2, w3, *refs):
    outs, (gathered, held, x_sems, w_sems) = refs[:4], refs[4:]
    tokens, own = same.shape[1], same.shape[2]
    n = same.shape[0]
    x, parity = at_ref[0], at_ref[1]
    nx = len(outs)
    copies = []
    for h in range(n):
        away = low.at[h] if h < n // 2 else high.at[h - n // 2]
        for i, (src, p) in enumerate(((same.at[h], parity), (away, 1 - parity))):
            to = pl.ds(pl.multiple_of((PARITIES * h + p) * own, own), own)
            copies.append(pltpu.make_async_copy(src, gathered.at[:, to], x_sems.at[i, h]))
    rows = PARITIES * n
    first = []
    for r in range(rows):
        src = weight.at[pl.ds(pl.multiple_of((r * nx + x) * own, own), own), :]
        first.append(pltpu.make_async_copy(src, held.at[0, r], w_sems.at[0, r]))
    others = [
        pltpu.make_async_copy(w, held.at[k + 1], w_sems.at[k + 1, 0]) for k, w in enumerate((w1, w2, w3))
    ]
    for c in copies + others + first:
        c.start()
    for c in copies:
        c.wait()
    for k in (1, 2, 3, 0):
        if k:
            others[k - 1].wait()
        else:
            for c in first:
                c.wait()
        w = held[k].reshape(rows * own, held.shape[3])
        for m in range(0, tokens, 256):
            outs[k][m : m + 256, :] = jnp.dot(
                gathered[m : m + 256, :], w, preferred_element_type=jnp.float32
            ).astype(outs[k].dtype)


def matmul(at, same, low, high, weight, ws):
    tokens, own = same.shape[1:]
    width = weight.shape[1]
    rows = PARITIES * same.shape[0]
    out = [
        jax.ShapeDtypeStruct((tokens, width), jnp.bfloat16 if k else jnp.float32)
        for k in range(4)
    ]
    return pl.pallas_call(
        matmul_kernel,
        out_shape=out,
        in_specs=[SMEM] + [ANY] * 7,
        out_specs=[VMEM] * 4,
        scratch_shapes=[
            pltpu.VMEM((tokens, rows * own), jnp.bfloat16),
            pltpu.VMEM((4, rows, own, width), jnp.bfloat16),
            pltpu.SemaphoreType.DMA((2, same.shape[0])),
            pltpu.SemaphoreType.DMA((4, rows)),
        ],
        compiler_params=params(16),
        cost_estimate=cost(6 * MIB, 2 * tokens * rows * own * width * 4),
    )(at, same, low, high, weight, *ws)


def last_kernel(low_ref, up_a_ref, up_b_ref, own_ref, r1_ref, r2_ref, r3_ref, out_ref):
    first = up_a_ref.shape[2] - out_ref.shape[1]
    each = RANK // PIECE
    for b in range(up_a_ref.shape[0]):
        rows = slice(b * BLOCK, (b + 1) * BLOCK)
        up = jnp.concatenate([up_a_ref[b, :, first:], up_b_ref[b, :, first:]], axis=0)
        shrunk = low_ref[b * each : (b + 1) * each].reshape(RANK, BLOCK)
        adapted = lax.dot_general(
            shrunk, up, (((0,), (0,)), ((), ())), preferred_element_type=jnp.float32
        )
        base = own_ref[rows, :]
        for r in (r1_ref, r2_ref, r3_ref):
            base = base + r[rows, :].astype(jnp.float32)
        out_ref[rows, :] = (base + adapter_scale * adapted).astype(out_ref.dtype)


def last(low, up_a, up_b, own, received):
    return pl.pallas_call(
        last_kernel,
        out_shape=jax.ShapeDtypeStruct(own.shape, jnp.bfloat16),
        in_specs=[VMEM] * 7,
        out_specs=VMEM,
        compiler_params=params(8),
        cost_estimate=cost(3 * MIB, 2 * own.size * RANK),
    )(low, up_a, up_b, own, *received)


def solution(mesh):
    tp, rep = mesh.shape["tp"], mesh.shape["rep"]
    nx = tp // NY
    names = ("z", "core", "yh", "yl", "x")
    grid = Mesh(
        mesh.devices.reshape(rep // CORES, CORES, NY // PARITIES, PARITIES, nx), names
    )
    reps, tps, ys = names[:2], names[2:], names[2:4]

    def shift(a, axis, size, by):
        return lax.ppermute(a, axis, [(i, (i + by) % size) for i in range(size)])

    def local(attn, weight, down, up, index, table):
        own, width = attn.shape[1], weight.shape[1]
        x, parity, core = (lax.axis_index(a).astype(jnp.int32) for a in ("x", "yl", "core"))

        pages = lax.all_to_all(pack(core[None], down, up, tp), tps, 0, 0, tiled=True)
        other_index = shift(index, "core", CORES, 1)

        same = lax.all_gather(attn, "yh")
        half = same.shape[0] // 2
        low_y = shift(same[:half], ys, NY, 1)
        high_y = shift(same[half:], ys, NY, -1)

        by_x = weight.reshape(NY, nx, own, width)
        ws = []
        for k in range(1, nx):
            mine = lax.dynamic_index_in_dim(by_x, (x + (nx - k)) % nx, 1, keepdims=False)
            ws.append(shift(mine, "x", nx, nx - k))

        mine, send = choose(index, other_index, table, pages)
        other = shift(send, "core", CORES, 1)
        pieces = shrink(attn, mine, other, tp)
        pieces = lax.all_to_all(pieces, tps, 0, 0, tiled=True)
        low = lax.all_to_all(total(pieces), tps, 0, 0, tiled=True)

        outs = matmul(jnp.stack([x, parity]), same, low_y, high_y, weight, ws)
        received = [shift(outs[k], "x", nx, k) for k in range(1, nx)]
        return last(low, mine, other, outs[0], received)

    return jax.shard_map(
        local,
        mesh=grid,
        in_specs=(P(reps, tps), P(None, tps), P(tps), P(tps), P(reps), P()),
        out_specs=P(reps, tps),
        check_vma=False,
    )
```

time: 220 us -> 109 us (0.50)
  blocking collectives: 159 us -> 22.2 us
  starting transfers between devices: 14.7 us -> 55.7 us
  between operations: 13.5 us -> 0.28 us
  Pallas kernels: 0 us -> 10.1 us
  matrix products: 7.64 us -> 0 us
  waiting for transfers between devices: 16.1 us -> 11.9 us
    dot_general x1 -> x0, blocking collectives: 159 us -> none  [reference(): jnp.einsum('btf,brf->brt', row_blocks, down_block_rows, precision=lax.Pre...]
    ppermute x0 -> x10, starting transfers between devices: none -> 32.8 us  [shift(): return lax.ppermute(a, axis, [(i, (i + by) % size) for i in range(size)])]
    all_to_all x0 -> x3, starting transfers between devices: none -> 22.9 us  [the longest x1 10.1 us: local(): lax.all_to_all(pack(core[None], down, up, tp), tps, 0, 0, tiled=True)]
    all_gather x0 -> x1, blocking collectives: none -> 22.2 us  [local(): same = lax.all_gather(attn, 'yh')]
    another operation x2 -> x0, waiting for transfers between devices: 15.4 us -> none
    another operation x2 -> x0, starting transfers between devices: 14.6 us -> none
    pallas_call x0 -> x6, Pallas kernels: none -> 10.1 us  [the longest x1 5.27 us: matmul(): pl.pallas_call(matmul_kernel, out_shape=out, in_specs=[SMEM] + [ANY] * 7,...]
    ppermute x0 -> x10, waiting for transfers between devices: none -> 8.89 us  [shift(): return lax.ppermute(a, axis, [(i, (i + by) % size) for i in range(size)])]
  transfers between devices with their start and end apart: 3 -> 13, of which waited for: 1 -> 4; matrix products, arithmetic and copies ran while one was open for 5% -> 2% of each run, Pallas kernels for 0% -> 7%
where the time goes in v1:
time: 109 us; the launch traced here: 108 us
  starting transfers between devices  55.7 us (51%)
  blocking collectives  22.2 us (20%)
  waiting for transfers between devices  11.9 us (11%)
  Pallas kernels  10.1 us (9%)
  local copies, waits for them, and re-layouts  7.76 us (7%)
    ppermute x10, starting transfers between devices, shift(): return lax.ppermute(a, axis, [(i, (i + by) % size) for i in range(size)])  32.8 us
    all_gather x1, blocking collectives, local(): same = lax.all_gather(attn, 'yh')  22.2 us
    all_to_all x1, starting transfers between devices, local(): lax.all_to_all(pack(core[None], down, up, tp), tps, 0, 0, tiled=True)  10.1 us
    ppermute x10, waiting for transfers between devices, shift(): return lax.ppermute(a, axis, [(i, (i + by) % size) for i in range(size)])  8.89 us
    all_to_all x1, starting transfers between devices, local(): pieces = lax.all_to_all(pieces, tps, 0, 0, tiled=True)  6.97 us
    all_to_all x1, starting transfers between devices, local(): low = lax.all_to_all(total(pieces), tps, 0, 0, tiled=True)  5.87 us
    unnamed x18, local copies, waits for them, and re-layouts  5.76 us
    pallas_call x1, Pallas kernels, matmul(): pl.pallas_call(matmul_kernel, out_shape=out, in_specs=[SMEM] + [ANY] * 7,...  5.27 us
  transfers between devices with their start and end apart: 13, of which 4 were waited for; matrix products, arithmetic and copies ran while one was open for 2% of the time, Pallas kernels for 7%

profile of v1, /device:TPU:64, one launch (start us, length us, event | category | flops | bytes accessed | tf_op | source)
XLA Modules:
  0.0 108.1 jit_solution(5485332077881337299)
XLA Ops:
  0.0 1.4 %copy-done.2 = bf16[1,64,8192]{2,1,0:T(8,128)(2,1)S(1)} copy-done((bf16[1,64,8192]{2,1,0:T(8,128)(2,1)S(1)}, bf16[1,64,8192]{2,1,0:T(8,128)(2,1)}, u32[]{:S(2)}) %copy-start.2) | copy-done | bytes 1048600
  3.5 10.1 %all-to-all-start = ((bf16[32,32,384]{2,1,0:T(8,128)(2,1)}), bf16[32,32,384]{2,1,0:T(8,128)(2,1)S(1)}, u32[]{:S(2)}, u32[]{:S(2)}) async-start(bf16[32,32,384]{2,1,0:T(8,128)(2,1)} %shard_map.64), calls=%async_computation | async-start | bytes 1572864 | tf_op jit(solution)/shard_map/all_to_all | solution.py:243
  13.7 1.2 %dynamic-slice_bitcast_fusion = (bf16[8,128,256]{2,1,0:T(8,128)(2,1)}, bf16[8,128,256]{2,1,0:T(8,128)(2,1)}, bf16[8,128,256]{2,1,0:T(8,128)(2,1)}) fusion(bf16[8,4,128,256]{3,2,1,0:T(8,128)(2,1)S(1)} %bitcast.20, s32[]{:T(128)S(6)} %select_n.30, s32[]{:T(128)S(6)} %select_n.28, s32[]{:T(128)S(6)} %select_n.26), kind=kLoop, calls=%fused_computation | loop fusion | bytes 3145740 | tf_op jit(solution)/shard_map/jit(dynamic_index_in_dim)/squeeze | solution.py:254
  14.9 4.9 %collective-permute-start.4 = (bf16[8,128,256]{2,1,0:T(8,128)(2,1)}, bf16[8,128,256]{2,1,0:T(8,128)(2,1)S(1)}, u32[]{:S(2)}, u32[]{:S(2)}) collective-permute-start(bf16[8,128,256]{2,1,0:T(8,128)(2,1)} %get-tuple-element.19), channel_id=1, source_target_pairs={{0,3},{1,0},{2,1},{3,2},{4,7},{5,4},{6,5},{7,6},{8,11},{9,8},{10,9... | collective-permute-start | bytes 1572872 | tf_op jit(solution)/shard_map/ppermute | solution.py:237
  19.8 2.8 %collective-permute-start.5 = (bf16[8,128,256]{2,1,0:T(8,128)(2,1)}, bf16[8,128,256]{2,1,0:T(8,128)(2,1)}, u32[]{:S(2)}, u32[]{:S(2)}) collective-permute-start(bf16[8,128,256]{2,1,0:T(8,128)(2,1)} %get-tuple-element.18), channel_id=1, source_target_pairs={{0,2},{1,3},{2,0},{3,1},{4,6},{5,7},{6,4},{7,5},{8,10},{9,11},{10,... | collective-permute-start | bytes 1572872 | tf_op jit(solution)/shard_map/ppermute | solution.py:237
  22.5 2.8 %collective-permute-start.6 = (bf16[8,128,256]{2,1,0:T(8,128)(2,1)}, bf16[8,128,256]{2,1,0:T(8,128)(2,1)}, u32[]{:S(2)}, u32[]{:S(2)}) collective-permute-start(bf16[8,128,256]{2,1,0:T(8,128)(2,1)} %get-tuple-element.17), channel_id=1, source_target_pairs={{0,1},{1,2},{2,3},{3,0},{4,5},{5,6},{6,7},{7,4},{8,9},{9,10},{10,1... | collective-permute-start | bytes 1572872 | tf_op jit(solution)/shard_map/ppermute | solution.py:237
  25.3 1.9 %collective-permute-start = (s32[6]{0:T(128)S(1)}, s32[6]{0:T(128)S(1)}, u32[]{:S(2)}, u32[]{:S(2)}) collective-permute-start(s32[6]{0:T(128)S(1)} %copy-done.5), channel_id=1, source_target_pairs={{0,32},{32,0},{1,33},{33,1},{2,34},{34,2},{3,35},{35,3},{4,36},{36... | collective-permute-start | bytes 80 | tf_op jit(solution)/shard_map/ppermute | solution.py:237
  27.3 22.2 %all-gather = bf16[3072,128]{1,0:T(8,128)(2,1)S(1)} all-gather(bf16[768,128]{1,0:T(8,128)(2,1)S(1)} %copy-done.3), channel_id=2, replica_groups=mesh['z'=8,'core'=2,'yh'=4,'yl'=2,'x'=4] {'yh'}, dimensions={0}, use_global_device_ids=true | all-gather | bytes 983040 | tf_op jit(solution)/shard_map/all_gather | solution.py:246
  49.5 1.1 shard_map.65
  50.6 1.9 %collective-permute-start.1 = (bf16[6,32,384]{2,1,0:T(8,128)(2,1)S(1)}, bf16[6,32,384]{2,1,0:T(8,128)(2,1)S(1)}, u32[]{:S(2)}, u32[]{:S(2)}) collective-permute-start(bf16[6,32,384]{2,1,0:T(8,128)(2,1)S(1)} %get-tuple-element.12), channel_id=1, source_target_pairs={{0,32},{32,0},{1,33},{33,1},{2,34},{34,2},{3,35},{35,3},{4,36},{36... | collective-permute-start | bytes 442376 | tf_op jit(solution)/shard_map/ppermute | solution.py:237
  53.3 1.9 %collective-permute-start.2 = (bf16[2,768,128]{2,1,0:T(8,128)(2,1)}, bf16[2,768,128]{2,1,0:T(8,128)(2,1)S(1)}, u32[]{:S(2)}, u32[]{:S(2)}) collective-permute-start(bf16[2,768,128]{2,1,0:T(8,128)(2,1)} %bitcast.4), channel_id=1, source_target_pairs={{0,4},{4,8},{8,12},{12,16},{16,20},{20,24},{24,28},{28,0},{1,5},{5... | collective-permute-start | bytes 1179656 | tf_op jit(solution)/shard_map/ppermute | solution.py:237
  55.2 5.1 %collective-permute-start.3 = (bf16[2,768,128]{2,1,0:T(8,128)(2,1)S(1)}, bf16[2,768,128]{2,1,0:T(8,128)(2,1)S(1)}, u32[]{:S(2)}, u32[]{:S(2)}) collective-permute-start(bf16[2,768,128]{2,1,0:T(8,128)(2,1)S(1)} %bitcast.21), channel_id=1, source_target_pairs={{0,28},{4,0},{8,4},{12,8},{16,12},{20,16},{24,20},{28,24},{1,29},{... | collective-permute-start | bytes 1179656 | tf_op jit(solution)/shard_map/ppermute | solution.py:237
  61.4 7.0 %all-to-all-start.1 = ((bf16[32,16,128]{2,1,0:T(8,128)(2,1)}), bf16[32,16,128]{2,1,0:T(8,128)(2,1)S(1)}, u32[]{:S(2)}, u32[]{:S(2)}) async-start(bf16[32,16,128]{2,1,0:T(8,128)(2,1)} %shard_map.66), calls=%async_computation.1 | async-start | bytes 262144 | tf_op jit(solution)/shard_map/all_to_all | solution.py:260
  68.4 1.3 %collective-permute-done.3.high = bf16[2,768,128]{2,1,0:T(8,128)(2,1)S(1)} collective-permute-done((bf16[2,768,128]{2,1,0:T(8,128)(2,1)S(1)}, bf16[2,768,128]{2,1,0:T(8,128)(2,1)S(1)}, u32[]{:S(2)}, u32[]{:S(2)}) %collective-permute-start.3) | collective-permute-done | bytes 393248 | tf_op jit(solution)/shard_map/ppermute | solution.py:237
  70.5 1.6 %copy-done.1 = bf16[4096,256]{1,0:T(8,128)(2,1)S(1)} copy-done((bf16[4096,256]{1,0:T(8,128)(2,1)S(1)}, bf16[4096,256]{1,0:T(8,128)(2,1)}, u32[]{:S(2)}) %copy-start.1) | copy-done | bytes 2097176
  73.0 5.3 %shard_map.68 = (f32[768,256]{1,0:T(8,128)S(1)}, bf16[768,256]{1,0:T(8,128)(2,1)}, bf16[768,256]{1,0:T(8,128)(2,1)}, bf16[768,256]{1,0:T(8,128)(2,1)}) custom-call(s32[2]{0:T(128)S(1)} %pad_add_fusion.at_ref, bf16[4,768,128]{2,1,0:T(8,128)(2,1)S(1)} %bitcast.19, bf16[2,768,128]{2,1,0:T(8,128)(2,1)S(1)} %collective-permute-done.2.low, ...), custom_call_target="tpu_custom_call" | custom-call | flops 1610612736 | bytes 6291456 | tf_op jit(solution)/shard_map/pallas_call | solution.py:184
  78.3 4.2 %collective-permute-start.7 = (bf16[768,256]{1,0:T(8,128)(2,1)}, bf16[768,256]{1,0:T(8,128)(2,1)S(1)}, u32[]{:S(2)}, u32[]{:S(2)}) collective-permute-start(bf16[768,256]{1,0:T(8,128)(2,1)} %get-tuple-element.14), channel_id=1, source_target_pairs={{0,1},{1,2},{2,3},{3,0},{4,5},{5,6},{6,7},{7,4},{8,9},{9,10},{10,1... | collective-permute-start | bytes 1179656 | tf_op jit(solution)/shard_map/ppermute | solution.py:237
  82.5 3.8 %collective-permute-start.8 = (bf16[768,256]{1,0:T(8,128)(2,1)}, bf16[768,256]{1,0:T(8,128)(2,1)S(1)}, u32[]{:S(2)}, u32[]{:S(2)}) collective-permute-start(bf16[768,256]{1,0:T(8,128)(2,1)} %get-tuple-element.15), channel_id=1, source_target_pairs={{0,2},{1,3},{2,0},{3,1},{4,6},{5,7},{6,4},{7,5},{8,10},{9,11},{10,... | collective-permute-start | bytes 1179656 | tf_op jit(solution)/shard_map/ppermute | solution.py:237
  86.3 3.5 %collective-permute-start.9 = (bf16[768,256]{1,0:T(8,128)(2,1)}, bf16[768,256]{1,0:T(8,128)(2,1)S(1)}, u32[]{:S(2)}, u32[]{:S(2)}) collective-permute-start(bf16[768,256]{1,0:T(8,128)(2,1)} %get-tuple-element.16), channel_id=1, source_target_pairs={{0,3},{1,0},{2,1},{3,2},{4,7},{5,4},{6,5},{7,6},{8,11},{9,8},{10,9... | collective-permute-start | bytes 1179656 | tf_op jit(solution)/shard_map/ppermute | solution.py:237
  90.6 5.9 %all-to-all-start.2 = ((bf16[32,16,128]{2,1,0:T(8,128)(2,1)}), bf16[32,16,128]{2,1,0:T(8,128)(2,1)S(1)}, u32[]{:S(2)}, u32[]{:S(2)}) async-start(bf16[32,16,128]{2,1,0:T(8,128)(2,1)} %shard_map.67), calls=%async_computation.2 | async-start | bytes 262144 | tf_op jit(solution)/shard_map/all_to_all | solution.py:261
  96.5 5.4 %collective-permute-done.8.r2_ref = bf16[768,256]{1,0:T(8,128)(2,1)S(1)} collective-permute-done((bf16[768,256]{1,0:T(8,128)(2,1)}, bf16[768,256]{1,0:T(8,128)(2,1)S(1)}, u32[]{:S(2)}, u32[]{:S(2)}) %collective-permute-start.8) | collective-permute-done | bytes 393248 | tf_op jit(solution)/shard_map/ppermute | solution.py:237
  101.8 2.1 %collective-permute-done.9.r3_ref = bf16[768,256]{1,0:T(8,128)(2,1)S(1)} collective-permute-done((bf16[768,256]{1,0:T(8,128)(2,1)}, bf16[768,256]{1,0:T(8,128)(2,1)S(1)}, u32[]{:S(2)}, u32[]{:S(2)}) %collective-permute-start.9) | collective-permute-done | bytes 393248 | tf_op jit(solution)/shard_map/ppermute | solution.py:237
  104.0 3.0 %all-to-all-done.2.low_ref = bf16[32,16,128]{2,1,0:T(8,128)(2,1)S(1)} async-done(((bf16[32,16,128]{2,1,0:T(8,128)(2,1)}), bf16[32,16,128]{2,1,0:T(8,128)(2,1)S(1)}, u32[]{:S(2)}, u32[]{:S(2)}) %all-to-all-start.2) | async-done | bytes 131104 | tf_op jit(solution)/shard_map/all_to_all | solution.py:261
  107.0 1.1 %shard_map.69 = bf16[768,256]{1,0:T(8,128)(2,1)} custom-call(bf16[32,16,128]{2,1,0:T(8,128)(2,1)S(1)} %all-to-all-done.2.low_ref, bf16[6,32,384]{2,1,0:T(8,128)(2,1)S(1)} %get-tuple-element.11.mine_ref.up_a_ref, bf16[6,32,384]{2,1,0:T(8,128)(2,1)S(1)} %collective-permute-done.1.other_ref.up_b_ref, f32[768,256]{1,0:T(8,128)S(1)} %get-tuple-element.13.own_ref, ...), custom_call_target="tpu_custom_call" | custom-call | flops 25165824 | bytes 3145728 | tf_op jit(solution)/shard_map/pallas_call | solution.py:217
  (30 shorter events, 6.4 us)
Async XLA Ops:
  0.0 13.7 %copy-start = (bf16[4096,256]{1,0:T(8,128)(2,1)S(1)}, bf16[4096,256]{1,0:T(8,128)(2,1)}, u32[]{:S(2)}) copy-start(bf16[4096,256]{1,0:T(8,128)(2,1)} %weight.1) | copy-start | bytes 6291460
  0.0 1.4 %copy-start.2 = (bf16[1,64,8192]{2,1,0:T(8,128)(2,1)S(1)}, bf16[1,64,8192]{2,1,0:T(8,128)(2,1)}, u32[]{:S(2)}) copy-start(bf16[1,64,8192]{2,1,0:T(8,128)(2,1)} %up_ref.1) | copy-start | bytes 3145732
  1.4 1.0 copy-start.4
  3.5 21.8 %copy-start.5 = (s32[6]{0:T(128)S(1)}, s32[6]{0:T(128)}, u32[]{:S(2)}) copy-start(s32[6]{0:T(128)} %index_ref.1) | copy-start | bytes 76
  3.5 23.8 %copy-start.3 = (bf16[768,128]{1,0:T(8,128)(2,1)S(1)}, bf16[768,128]{1,0:T(8,128)(2,1)}, u32[]{:S(2)}) copy-start(bf16[768,128]{1,0:T(8,128)(2,1)} %attn_ref.1) | copy-start | bytes 589828
  3.5 46.0 %all-to-all-start = ((bf16[32,32,384]{2,1,0:T(8,128)(2,1)}), bf16[32,32,384]{2,1,0:T(8,128)(2,1)S(1)}, u32[]{:S(2)}, u32[]{:S(2)}) async-start(bf16[32,32,384]{2,1,0:T(8,128)(2,1)} %shard_map.64), calls=%async_computation | async-start | bytes 1572864 | tf_op jit(solution)/shard_map/all_to_all | solution.py:243
  13.6 35.9 %copy-start.6 = (s32[32]{0:T(128)S(1)}, s32[32]{0:T(128)}, u32[]{:S(2)}) copy-start(s32[32]{0:T(128)} %table_ref.1) | copy-start | bytes 388
  14.9 55.6 %collective-permute-start.4 = (bf16[8,128,256]{2,1,0:T(8,128)(2,1)}, bf16[8,128,256]{2,1,0:T(8,128)(2,1)S(1)}, u32[]{:S(2)}, u32[]{:S(2)}) collective-permute-start(bf16[8,128,256]{2,1,0:T(8,128)(2,1)} %get-tuple-element.19), channel_id=1, source_target_pairs={{0,3},{1,0},{2,1},{3,2},{4,7},{5,4},{6,5},{7,6},{8,11},{9,8},{10,9... | collective-permute-start | bytes 1572872 | tf_op jit(solution)/shard_map/ppermute | solution.py:237
  19.8 50.7 %collective-permute-start.5 = (bf16[8,128,256]{2,1,0:T(8,128)(2,1)}, bf16[8,128,256]{2,1,0:T(8,128)(2,1)}, u32[]{:S(2)}, u32[]{:S(2)}) collective-permute-start(bf16[8,128,256]{2,1,0:T(8,128)(2,1)} %get-tuple-element.18), channel_id=1, source_target_pairs={{0,2},{1,3},{2,0},{3,1},{4,6},{5,7},{6,4},{7,5},{8,10},{9,11},{10,... | collective-permute-start | bytes 1572872 | tf_op jit(solution)/shard_map/ppermute | solution.py:237
  22.5 47.9 %collective-permute-start.6 = (bf16[8,128,256]{2,1,0:T(8,128)(2,1)}, bf16[8,128,256]{2,1,0:T(8,128)(2,1)}, u32[]{:S(2)}, u32[]{:S(2)}) collective-permute-start(bf16[8,128,256]{2,1,0:T(8,128)(2,1)} %get-tuple-element.17), channel_id=1, source_target_pairs={{0,1},{1,2},{2,3},{3,0},{4,5},{5,6},{6,7},{7,4},{8,9},{9,10},{10,1... | collective-permute-start | bytes 1572872 | tf_op jit(solution)/shard_map/ppermute | solution.py:237
  25.3 24.2 %collective-permute-start = (s32[6]{0:T(128)S(1)}, s32[6]{0:T(128)S(1)}, u32[]{:S(2)}, u32[]{:S(2)}) collective-permute-start(s32[6]{0:T(128)S(1)} %copy-done.5), channel_id=1, source_target_pairs={{0,32},{32,0},{1,33},{33,1},{2,34},{34,2},{3,35},{35,3},{4,36},{36... | collective-permute-start | bytes 80 | tf_op jit(solution)/shard_map/ppermute | solution.py:237
  50.6 4.6 %collective-permute-start.1 = (bf16[6,32,384]{2,1,0:T(8,128)(2,1)S(1)}, bf16[6,32,384]{2,1,0:T(8,128)(2,1)S(1)}, u32[]{:S(2)}, u32[]{:S(2)}) collective-permute-start(bf16[6,32,384]{2,1,0:T(8,128)(2,1)S(1)} %get-tuple-element.12), channel_id=1, source_target_pairs={{0,32},{32,0},{1,33},{33,1},{2,34},{34,2},{3,35},{35,3},{4,36},{36... | collective-permute-start | bytes 442376 | tf_op jit(solution)/shard_map/ppermute | solution.py:237
  53.3 15.0 %collective-permute-start.2 = (bf16[2,768,128]{2,1,0:T(8,128)(2,1)}, bf16[2,768,128]{2,1,0:T(8,128)(2,1)S(1)}, u32[]{:S(2)}, u32[]{:S(2)}) collective-permute-start(bf16[2,768,128]{2,1,0:T(8,128)(2,1)} %bitcast.4), channel_id=1, source_target_pairs={{0,4},{4,8},{8,12},{12,16},{16,20},{20,24},{24,28},{28,0},{1,5},{5... | collective-permute-start | bytes 1179656 | tf_op jit(solution)/shard_map/ppermute | solution.py:237
  55.2 14.5 %collective-permute-start.3 = (bf16[2,768,128]{2,1,0:T(8,128)(2,1)S(1)}, bf16[2,768,128]{2,1,0:T(8,128)(2,1)S(1)}, u32[]{:S(2)}, u32[]{:S(2)}) collective-permute-start(bf16[2,768,128]{2,1,0:T(8,128)(2,1)S(1)} %bitcast.21), channel_id=1, source_target_pairs={{0,28},{4,0},{8,4},{12,8},{16,12},{20,16},{24,20},{28,24},{1,29},{... | collective-permute-start | bytes 1179656 | tf_op jit(solution)/shard_map/ppermute | solution.py:237
  61.4 28.5 %all-to-all-start.1 = ((bf16[32,16,128]{2,1,0:T(8,128)(2,1)}), bf16[32,16,128]{2,1,0:T(8,128)(2,1)S(1)}, u32[]{:S(2)}, u32[]{:S(2)}) async-start(bf16[32,16,128]{2,1,0:T(8,128)(2,1)} %shard_map.66), calls=%async_computation.1 | async-start | bytes 262144 | tf_op jit(solution)/shard_map/all_to_all | solution.py:260
  69.7 0.7 copy-start.7
  70.5 1.6 %copy-start.1 = (bf16[4096,256]{1,0:T(8,128)(2,1)S(1)}, bf16[4096,256]{1,0:T(8,128)(2,1)}, u32[]{:S(2)}) copy-start(bf16[4096,256]{1,0:T(8,128)(2,1)} %weight.1) | copy-start | bytes 6291460
  72.1 1.0 copy-start.8
  78.3 18.1 %collective-permute-start.7 = (bf16[768,256]{1,0:T(8,128)(2,1)}, bf16[768,256]{1,0:T(8,128)(2,1)S(1)}, u32[]{:S(2)}, u32[]{:S(2)}) collective-permute-start(bf16[768,256]{1,0:T(8,128)(2,1)} %get-tuple-element.14), channel_id=1, source_target_pairs={{0,1},{1,2},{2,3},{3,0},{4,5},{5,6},{6,7},{7,4},{8,9},{9,10},{10,1... | collective-permute-start | bytes 1179656 | tf_op jit(solution)/shard_map/ppermute | solution.py:237
  82.5 19.3 %collective-permute-start.8 = (bf16[768,256]{1,0:T(8,128)(2,1)}, bf16[768,256]{1,0:T(8,128)(2,1)S(1)}, u32[]{:S(2)}, u32[]{:S(2)}) collective-permute-start(bf16[768,256]{1,0:T(8,128)(2,1)} %get-tuple-element.15), channel_id=1, source_target_pairs={{0,2},{1,3},{2,0},{3,1},{4,6},{5,7},{6,4},{7,5},{8,10},{9,11},{10,... | collective-permute-start | bytes 1179656 | tf_op jit(solution)/shard_map/ppermute | solution.py:237
  86.3 17.7 %collective-permute-start.9 = (bf16[768,256]{1,0:T(8,128)(2,1)}, bf16[768,256]{1,0:T(8,128)(2,1)S(1)}, u32[]{:S(2)}, u32[]{:S(2)}) collective-permute-start(bf16[768,256]{1,0:T(8,128)(2,1)} %get-tuple-element.16), channel_id=1, source_target_pairs={{0,3},{1,0},{2,1},{3,2},{4,7},{5,4},{6,5},{7,6},{8,11},{9,8},{10,9... | collective-permute-start | bytes 1179656 | tf_op jit(solution)/shard_map/ppermute | solution.py:237
  90.6 16.4 %all-to-all-start.2 = ((bf16[32,16,128]{2,1,0:T(8,128)(2,1)}), bf16[32,16,128]{2,1,0:T(8,128)(2,1)S(1)}, u32[]{:S(2)}, u32[]{:S(2)}) async-start(bf16[32,16,128]{2,1,0:T(8,128)(2,1)} %shard_map.67), calls=%async_computation.2 | async-start | bytes 262144 | tf_op jit(solution)/shard_map/all_to_all | solution.py:261

commit v2 on v0

v2 whole, which is shorter than its diff:
```python
import functools

import jax
import jax.numpy as jnp
from jax import lax
from jax.experimental import pallas as pl
from jax.experimental.pallas import tpu as pltpu
from jax.sharding import Mesh, PartitionSpec as P

RANK = 64
BLOCK = 128
NY, PARITIES = 8, 2
CORES = 2
PIECE = 16
adapter_scale = 2.0
MIB = 1 << 20
WHOLE = 60

VMEM = pl.BlockSpec(memory_space=pltpu.VMEM)
SMEM = pl.BlockSpec(memory_space=pltpu.SMEM)
ANY = pl.BlockSpec(memory_space=pl.ANY)


def cost(nbytes, flops=0):
    return pl.CostEstimate(flops=flops, transcendentals=0, bytes_accessed=nbytes)


def params(mib):
    return pltpu.CompilerParams(vmem_limit_bytes=mib * MIB)


def pack_kernel(down_ref, out_ref, held, sem):
    copy = pltpu.make_async_copy(down_ref.at[0], held, sem)
    copy.start()
    copy.wait()
    own = out_ref.shape[2]
    for d in range(out_ref.shape[0]):
        out_ref[d] = held[:, d * own : (d + 1) * own]


def pack(down, tp):
    return pl.pallas_call(
        pack_kernel,
        out_shape=jax.ShapeDtypeStruct((tp, RANK, down.shape[2] // tp), down.dtype),
        in_specs=[ANY],
        out_specs=VMEM,
        scratch_shapes=[pltpu.VMEM(down.shape[1:], down.dtype), pltpu.SemaphoreType.DMA],
        compiler_params=params(WHOLE),
        cost_estimate=cost(MIB),
    )(down)


def shrink_kernel(index_ref, table_ref, attn_ref, pages_ref, out_ref):
    blocks = index_ref.shape[0]
    each = RANK // PIECE
    for b in range(blocks):
        shrunk = lax.dot_general(
            pages_ref[table_ref[index_ref[b]]],
            attn_ref[b * BLOCK : (b + 1) * BLOCK, :],
            (((1,), (1,)), ((), ())),
            preferred_element_type=jnp.float32,
        ).astype(out_ref.dtype)
        out_ref[b * each : (b + 1) * each] = shrunk.reshape(each, PIECE, BLOCK)
    rest = out_ref.shape[0] - blocks * each
    if rest:
        out_ref[blocks * each :] = jnp.zeros((rest, PIECE, BLOCK), out_ref.dtype)


def shrink(index, table, attn, pages):
    return pl.pallas_call(
        shrink_kernel,
        out_shape=jax.ShapeDtypeStruct((pages.shape[0], PIECE, BLOCK), jnp.bfloat16),
        in_specs=[SMEM, SMEM, VMEM, VMEM],
        out_specs=VMEM,
        compiler_params=params(8),
        cost_estimate=cost(MIB // 2, 2 * attn.size * RANK),
    )(index, table, attn, pages)


def choose_kernel(index_ref, other_ref, table_ref, pages_ref, own_ref, send_ref, sems):
    n = own_ref.shape[0]
    copies = []
    for i, (who, out) in enumerate(((other_ref, send_ref), (index_ref, own_ref))):
        for b in range(n):
            src = pages_ref.at[table_ref[who[b]], pl.ds(PIECE, RANK), :]
            copies.append(pltpu.make_async_copy(src, out.at[b], sems.at[i, b]))
    for c in copies:
        c.start()
    for c in copies:
        c.wait()


def choose(index, other, table, pages):
    shape = jax.ShapeDtypeStruct((index.shape[0], RANK, pages.shape[2]), pages.dtype)
    return pl.pallas_call(
        choose_kernel,
        out_shape=[shape, shape],
        in_specs=[SMEM, SMEM, SMEM, ANY],
        out_specs=[VMEM, VMEM],
        scratch_shapes=[pltpu.SemaphoreType.DMA((2, index.shape[0]))],
        compiler_params=params(8),
        cost_estimate=cost(MIB // 2),
    )(index, other, table, pages)


def total_kernel(core_ref, in_ref, up_ref, out_ref, up, sem):
    ranks = up.shape[0]
    rows = pl.ds(pl.multiple_of(core_ref[0] * ranks, ranks), ranks)
    copy = pltpu.make_async_copy(up_ref.at[0, rows, :], up, sem)
    copy.start()
    summed = jnp.sum(in_ref[...].astype(jnp.float32), axis=0).astype(out_ref.dtype)
    n, _, own = out_ref.shape
    copy.wait()
    for d in range(n):
        out_ref[d, :PIECE, :] = summed
        for i in range(CORES):
            at = PIECE + i * ranks
            out_ref[d, at : at + ranks, :] = up[:, (CORES * d + i) * own : (CORES * d + i + 1) * own]


def total(core, pieces, up):
    tp, _, own = pieces.shape
    return pl.pallas_call(
        total_kernel,
        out_shape=jax.ShapeDtypeStruct((tp, PIECE + RANK, own), pieces.dtype),
        in_specs=[SMEM, VMEM, ANY],
        out_specs=VMEM,
        scratch_shapes=[pltpu.VMEM((RANK // CORES, up.shape[2]), up.dtype), pltpu.SemaphoreType.DMA],
        compiler_params=params(8),
        cost_estimate=cost(MIB),
    )(core, pieces, up)


def product_kernel(n, parts, parity_ref, x_ref, *refs):
    offsets = [o for p in parts for o in p]
    xs, weights, outs = refs[: len(parts)], refs[len(parts) : len(parts) + n], refs[len(parts) + n : len(parts) + 2 * n]
    gathered, held, x_sems, w_sems = refs[len(parts) + 2 * n :]
    parity = parity_ref[0]
    ny, own = held.shape[1], held.shape[2]
    at, copies = 0, []
    for i, (x, p) in enumerate(zip(xs, parts)):
        to = gathered.at[at] if len(x.shape) == 2 else gathered.at[pl.ds(at, len(p))]
        copies.append(pltpu.make_async_copy(x, to, x_sems.at[i]))
        at += len(p)
    into = []
    for k, w in enumerate(weights):
        if len(w.shape) == 3:
            into.append([pltpu.make_async_copy(w, held.at[k], w_sems.at[k, 0])])
        else:
            nx = w.shape[0] // (ny * own)
            into.append([])
            for r in range(ny):
                rows = pl.ds(pl.multiple_of((r * nx + x_ref[0]) * own, own), own)
                into[-1].append(pltpu.make_async_copy(w.at[rows, :], held.at[k, r], w_sems.at[k, r]))
    for c in (*copies, *[c for group in into for c in group]):
        c.start()
    for c in copies:
        c.wait()
    for k in range(n):
        for c in into[k]:
            c.wait()
        w = jnp.concatenate([held[k, o + (1 - parity if p else parity)] for p, o in offsets], axis=0)
        for m in range(0, gathered.shape[1], 256):
            rows = slice(m, m + 256)
            x = jnp.concatenate([gathered[j, rows, :] for j in range(ny)], axis=1)
            outs[k][rows, :] = jnp.dot(x, w, preferred_element_type=jnp.float32).astype(outs[k].dtype)


def product(scalars, gathered, parts, weights, dtypes):
    n = len(weights)
    tokens, own = gathered[0].shape[-2:]
    ny = sum(len(p) for p in parts)
    width = weights[0].shape[-1]
    return pl.pallas_call(
        functools.partial(product_kernel, n, parts),
        out_shape=[jax.ShapeDtypeStruct((tokens, width), d) for d in dtypes],
        in_specs=[SMEM] * 2 + [ANY] * (len(gathered) + n),
        out_specs=[VMEM] * n,
        scratch_shapes=[
            pltpu.VMEM((ny, tokens, own), gathered[0].dtype),
            pltpu.VMEM((n, ny, own, width), weights[0].dtype),
            pltpu.SemaphoreType.DMA((len(gathered),)),
            pltpu.SemaphoreType.DMA((n, ny)),
        ],
        compiler_params=params(WHOLE),
        cost_estimate=cost(2 * n * MIB, 2 * tokens * ny * own * width * n),
    )(*scalars, *gathered, *weights)


def last_kernel(core_ref, low_ref, mine_ref, other_ref, own_hbm, r1_ref, r2_ref, r3_ref, out_ref, own_ref, sem):
    copy = pltpu.make_async_copy(own_hbm, own_ref, sem)
    copy.start()
    core = core_ref[0]
    half = RANK // CORES
    each = half // PIECE
    for b in range(mine_ref.shape[0]):
        rows = slice(b * BLOCK, (b + 1) * BLOCK)
        up = jnp.concatenate(
            [
                jnp.concatenate([r[b, i * half : (i + 1) * half, :] for i in range(CORES)], axis=1)
                for r in (mine_ref, other_ref)
            ],
            axis=0,
        )
        at = b * CORES * each
        shrunk = jnp.concatenate(
            [low_ref[pl.ds(at + c * each, each), :PIECE, :].reshape(half, BLOCK) for c in (core, 1 - core)], axis=0
        )
        adapted = lax.dot_general(
            shrunk, up, (((0,), (0,)), ((), ())), preferred_element_type=jnp.float32
        )
        if b == 0:
            copy.wait()
        base = own_ref[rows, :]
        for r in (r1_ref, r2_ref, r3_ref):
            base = base + r[rows, :].astype(jnp.float32)
        out_ref[rows, :] = (base + adapter_scale * adapted).astype(out_ref.dtype)


def last(core, low, mine, other, own, received):
    return pl.pallas_call(
        last_kernel,
        out_shape=jax.ShapeDtypeStruct(own.shape, jnp.bfloat16),
        in_specs=[SMEM] + [VMEM] * 3 + [ANY] + [VMEM] * 3,
        out_specs=VMEM,
        scratch_shapes=[pltpu.VMEM(own.shape, own.dtype), pltpu.SemaphoreType.DMA],
        compiler_params=params(8),
        cost_estimate=cost(3 * MIB, 2 * own.size * RANK),
    )(core, low, mine, other, own, *received)


def solution(mesh):
    tp, rep = mesh.shape["tp"], mesh.shape["rep"]
    ny, nx = NY, tp // NY
    names = ("z", "core", "yh", "yl", "x")
    grid = Mesh(mesh.devices.reshape(rep // CORES, CORES, ny // PARITIES, PARITIES, nx), names)
    reps, tps, ys = names[:2], names[2:], names[2:4]

    def shift(a, axis, size, by):
        return lax.ppermute(a, axis, [(i, (i + by) % size) for i in range(size)])

    def local(attn, weight, down, up, index, table):
        own, width = attn.shape[1], weight.shape[1]
        x, parity, core = (lax.axis_index(a).astype(jnp.int32) for a in ("x", "yl", "core"))
        scalars = (parity[None], x[None])

        pages = lax.all_to_all(pack(down, tp), tps, 0, 0, tiled=True)

        same = lax.all_gather(attn, "yh")
        pages, same = lax.optimization_barrier((pages, same))
        half = same.shape[0] // 2
        low_y = shift(same[:half], ys, ny, 1)
        high_y = shift(same[half:], ys, ny, -1)
        gathered = (same, low_y, high_y)
        parts = tuple(
            tuple((p, PARITIES * h) for h in hs)
            for p, hs in ((0, range(2 * half)), (1, range(half)), (1, range(half, 2 * half)))
        )

        by_x = weight.reshape(ny, nx, own, width)
        ws = [
            lax.dynamic_index_in_dim(by_x, (x + (nx - k)) % nx, 1, keepdims=False)
            for k in range(1, nx)
        ]
        ws = [shift(w, "x", nx, nx - k) for k, w in enumerate(ws, 1)]

        pieces = shrink(index, table, attn, pages)
        pieces = lax.all_to_all(pieces, tps, 0, 0, tiled=True)

        *outs, mid = product(
            scalars, gathered, parts, [*ws, weight], [jnp.bfloat16] * len(ws) + [jnp.float32]
        )
        pieces = lax.optimization_barrier((pieces, outs))[0]
        summed = total(core[None], pieces, up)
        low = lax.all_to_all(summed, tps, 0, 0, tiled=True)
        received = [shift(o, "x", nx, k) for k, o in enumerate(outs, 1)]

        index, _ = lax.optimization_barrier((index, (summed, outs)))
        other_index = shift(index, "core", CORES, 1)
        mine, send = choose(index, other_index, table, low)
        other = shift(send, "core", CORES, 1)
        return last(core[None], low, mine, other, mid, received)

    return jax.shard_map(
        local,
        mesh=grid,
        in_specs=(P(reps, tps), P(None, tps), P(tps), P(tps), P(reps), P()),
        out_specs=P(reps, tps),
        check_vma=False,
    )
```

time: 220 us -> 104 us (0.47)
  the two profiles are of different devices: /device:TPU:64 before, /device:TPU:387 now
where the time goes in v2:
time: 104 us
  starting transfers between devices  61.5 us (59%)
  blocking collectives  18 us (17%)
  Pallas kernels  13 us (12%)
  waiting for transfers between devices  8.7 us (8%)
  local copies, waits for them, and re-layouts  1.98 us (2%)
    ppermute x10, starting transfers between devices, shift(): return lax.ppermute(a, axis, [(i, (i + by) % size) for i in range(size)])  36.9 us
    all_gather x1, blocking collectives, local(): same = lax.all_gather(attn, 'yh')  18 us
    all_to_all x1, starting transfers between devices, local(): pages = lax.all_to_all(pack(down, tp), tps, 0, 0, tiled=True)  9.83 us
    all_to_all x1, starting transfers between devices, local(): low = lax.all_to_all(summed, tps, 0, 0, tiled=True)  8.14 us
    ppermute x10, waiting for transfers between devices, shift(): return lax.ppermute(a, axis, [(i, (i + by) % size) for i in range(size)])  7.58 us
    all_to_all x1, starting transfers between devices, local(): pieces = lax.all_to_all(pieces, tps, 0, 0, tiled=True)  6.6 us
    pallas_call x1, Pallas kernels, product(): pl.pallas_call(functools.partial(product_kernel, n, parts), out_shape=[ja...  6.15 us
    pallas_call x1, Pallas kernels, pack(): pl.pallas_call(pack_kernel, out_shape=jax.ShapeDtypeStruct((tp, RANK, dow...  2.09 us
  transfers between devices with their start and end apart: 13, of which 3 were waited for; matrix products, arithmetic and copies ran while one was open for 1% of the time, Pallas kernels for 8%

profile of v2, /device:TPU:387, one launch (start us, length us, event | category | flops | bytes accessed | tf_op | source)
XLA Modules:
  0.0 103.5 jit_solution(18151960534437430346)
XLA Ops:
  0.0 2.1 %shard_map.64 = bf16[32,64,128]{2,1,0:T(8,128)(2,1)} custom-call(bf16[1,64,4096]{2,1,0:T(8,128)(2,1)} %down_ref.1), custom_call_target="tpu_custom_call" | custom-call | bytes 1048576 | tf_op jit(solution)/shard_map/pallas_call | solution.py:42
  2.1 9.8 %all-to-all-start = ((bf16[32,64,128]{2,1,0:T(8,128)(2,1)}), bf16[32,64,128]{2,1,0:T(8,128)(2,1)S(1)}, u32[]{:S(2)}, u32[]{:S(2)}) async-start(bf16[32,64,128]{2,1,0:T(8,128)(2,1)} %shard_map.64), calls=%async_computation | async-start | bytes 1048576 | tf_op jit(solution)/shard_map/all_to_all | solution.py:247
  12.0 1.1 %dynamic-slice_bitcast_fusion = (bf16[8,128,256]{2,1,0:T(8,128)(2,1)}, bf16[8,128,256]{2,1,0:T(8,128)(2,1)}, bf16[8,128,256]{2,1,0:T(8,128)(2,1)S(1)}) fusion(bf16[8,4,128,256]{3,2,1,0:T(8,128)(2,1)S(1)} %bitcast.19, s32[]{:T(128)S(6)} %select_n.30, s32[]{:T(128)S(6)} %select_n.28, s32[]{:T(128)S(6)} %select_n.26), kind=kLoop, calls=%fused_computation | loop fusion | bytes 3145740 | tf_op jit(solution)/shard_map/jit(dynamic_index_in_dim)/squeeze | solution.py:262
  13.2 3.1 %collective-permute-start.4 = (bf16[8,128,256]{2,1,0:T(8,128)(2,1)}, bf16[8,128,256]{2,1,0:T(8,128)(2,1)S(1)}, u32[]{:S(2)}, u32[]{:S(2)}) collective-permute-start(bf16[8,128,256]{2,1,0:T(8,128)(2,1)} %get-tuple-element.25), channel_id=1, source_target_pairs={{0,1},{1,2},{2,3},{3,0},{4,5},{5,6},{6,7},{7,4},{8,9},{9,10},{10,1... | collective-permute-start | bytes 1572872 | tf_op jit(solution)/shard_map/ppermute | solution.py:240
  16.3 2.8 %collective-permute-start.3 = (bf16[8,128,256]{2,1,0:T(8,128)(2,1)}, bf16[8,128,256]{2,1,0:T(8,128)(2,1)}, u32[]{:S(2)}, u32[]{:S(2)}) collective-permute-start(bf16[8,128,256]{2,1,0:T(8,128)(2,1)} %get-tuple-element.26), channel_id=1, source_target_pairs={{0,2},{1,3},{2,0},{3,1},{4,6},{5,7},{6,4},{7,5},{8,10},{9,11},{10,... | collective-permute-start | bytes 1572872 | tf_op jit(solution)/shard_map/ppermute | solution.py:240
  19.0 3.7 %collective-permute-start.2 = (bf16[8,128,256]{2,1,0:T(8,128)(2,1)S(1)}, bf16[8,128,256]{2,1,0:T(8,128)(2,1)}, u32[]{:S(2)}, u32[]{:S(2)}) collective-permute-start(bf16[8,128,256]{2,1,0:T(8,128)(2,1)S(1)} %get-tuple-element.27), channel_id=1, source_target_pairs={{0,3},{1,0},{2,1},{3,2},{4,7},{5,4},{6,5},{7,6},{8,11},{9,8},{10,9... | collective-permute-start | bytes 1572872 | tf_op jit(solution)/shard_map/ppermute | solution.py:240
  22.8 18.0 %all-gather = bf16[3072,128]{1,0:T(8,128)(2,1)S(1)} all-gather(bf16[768,128]{1,0:T(8,128)(2,1)S(1)} %copy-done.2), channel_id=2, replica_groups=mesh['z'=8,'core'=2,'yh'=4,'yl'=2,'x'=4] {'yh'}, dimensions={0}, use_global_device_ids=true | all-gather | bytes 983040 | tf_op jit(solution)/shard_map/all_gather | solution.py:249
  40.8 3.5 %collective-permute-start.1 = (bf16[2,768,128]{2,1,0:T(8,128)(2,1)S(1)}, bf16[2,768,128]{2,1,0:T(8,128)(2,1)}, u32[]{:S(2)}, u32[]{:S(2)}) collective-permute-start(bf16[2,768,128]{2,1,0:T(8,128)(2,1)S(1)} %get-tuple-element.28), channel_id=1, source_target_pairs={{0,28},{4,0},{8,4},{12,8},{16,12},{20,16},{24,20},{28,24},{1,29},{... | collective-permute-start | bytes 1179656 | tf_op jit(solution)/shard_map/ppermute | solution.py:240
  44.3 1.9 %collective-permute-start = (bf16[2,768,128]{2,1,0:T(8,128)(2,1)S(1)}, bf16[2,768,128]{2,1,0:T(8,128)(2,1)}, u32[]{:S(2)}, u32[]{:S(2)}) collective-permute-start(bf16[2,768,128]{2,1,0:T(8,128)(2,1)S(1)} %get-tuple-element.29), channel_id=1, source_target_pairs={{0,4},{4,8},{8,12},{12,16},{16,20},{20,24},{24,28},{28,0},{1,5},{5... | collective-permute-start | bytes 1179656 | tf_op jit(solution)/shard_map/ppermute | solution.py:240
  46.3 1.5 %shard_map.65 = bf16[32,16,128]{2,1,0:T(8,128)(2,1)} custom-call(s32[6]{0:T(128)S(1)} %copy-done.3, s32[32]{0:T(128)S(1)} %copy-done.4, bf16[768,128]{1,0:T(8,128)(2,1)S(1)} %copy-done.2, bf16[32,64,128]{2,1,0:T(8,128)(2,1)S(1)} %all-to-all-done.pages_ref), custom_call_target="tpu_custom_call" | custom-call | flops 12582912 | bytes 524288 | tf_op jit(solution)/shard_map/pallas_call | solution.py:70
  47.7 6.6 %all-to-all-start.1 = ((bf16[32,16,128]{2,1,0:T(8,128)(2,1)}), bf16[32,16,128]{2,1,0:T(8,128)(2,1)S(1)}, u32[]{:S(2)}, u32[]{:S(2)}) async-start(bf16[32,16,128]{2,1,0:T(8,128)(2,1)} %shard_map.65), calls=%async_computation.1 | async-start | bytes 262144 | tf_op jit(solution)/shard_map/all_to_all | solution.py:268
  55.1 6.2 %shard_map.66 = (bf16[768,256]{1,0:T(8,128)(2,1)}, bf16[768,256]{1,0:T(8,128)(2,1)}, bf16[768,256]{1,0:T(8,128)(2,1)}, f32[768,256]{1,0:T(8,128)}) custom-call(s32[1]{0:T(128)} %bitcast.2.parity_ref, s32[1]{0:T(128)} %bitcast.3.x_ref, bf16[4,768,128]{2,1,0:T(8,128)(2,1)} %bitcast.18, bf16[2,768,128]{2,1,0:T(8,128)(2,1)} %collective-permute-done.refs_1_, ...), custom_call_target="tpu_custom_call" | custom-call | flops 1610612736 | bytes 8388608 | tf_op jit(solution)/shard_map/pallas_call | solution.py:174
  61.3 1.1 %all-to-all-done.1.in_ref = bf16[32,16,128]{2,1,0:T(8,128)(2,1)S(1)} async-done(((bf16[32,16,128]{2,1,0:T(8,128)(2,1)}), bf16[32,16,128]{2,1,0:T(8,128)(2,1)S(1)}, u32[]{:S(2)}, u32[]{:S(2)}) %all-to-all-start.1) | async-done | bytes 131104 | tf_op jit(solution)/shard_map/all_to_all | solution.py:268
  62.5 1.0 shard_map.67
  63.5 8.1 %all-to-all-start.2 = ((bf16[32,80,128]{2,1,0:T(8,128)(2,1)}), bf16[32,80,128]{2,1,0:T(8,128)(2,1)S(1)}, u32[]{:S(2)}, u32[]{:S(2)}) async-start(bf16[32,80,128]{2,1,0:T(8,128)(2,1)} %shard_map.67), calls=%async_computation.2 | async-start | bytes 1310720 | tf_op jit(solution)/shard_map/all_to_all | solution.py:275
  71.6 3.1 %collective-permute-start.7 = (bf16[768,256]{1,0:T(8,128)(2,1)}, bf16[768,256]{1,0:T(8,128)(2,1)S(1)}, u32[]{:S(2)}, u32[]{:S(2)}) collective-permute-start(bf16[768,256]{1,0:T(8,128)(2,1)} %get-tuple-element.17), channel_id=1, source_target_pairs={{0,1},{1,2},{2,3},{3,0},{4,5},{5,6},{6,7},{7,4},{8,9},{9,10},{10,1... | collective-permute-start | bytes 1179656 | tf_op jit(solution)/shard_map/ppermute | solution.py:240
  74.7 2.7 %collective-permute-start.8 = (bf16[768,256]{1,0:T(8,128)(2,1)S(1)}, bf16[768,256]{1,0:T(8,128)(2,1)S(1)}, u32[]{:S(2)}, u32[]{:S(2)}) collective-permute-start(bf16[768,256]{1,0:T(8,128)(2,1)S(1)} %copy-done.9), channel_id=1, source_target_pairs={{0,2},{1,3},{2,0},{3,1},{4,6},{5,7},{6,4},{7,5},{8,10},{9,11},{10,... | collective-permute-start | bytes 1179656 | tf_op jit(solution)/shard_map/ppermute | solution.py:240
  77.5 3.7 %collective-permute-start.9 = (bf16[768,256]{1,0:T(8,128)(2,1)S(1)}, bf16[768,256]{1,0:T(8,128)(2,1)S(1)}, u32[]{:S(2)}, u32[]{:S(2)}) collective-permute-start(bf16[768,256]{1,0:T(8,128)(2,1)S(1)} %copy-done.8), channel_id=1, source_target_pairs={{0,3},{1,0},{2,1},{3,2},{4,7},{5,4},{6,5},{7,6},{8,11},{9,8},{10,9... | collective-permute-start | bytes 1179656 | tf_op jit(solution)/shard_map/ppermute | solution.py:240
  81.2 8.3 %collective-permute-start.5 = (s32[6]{0:T(128)S(1)}, s32[6]{0:T(128)S(1)}, u32[]{:S(2)}, u32[]{:S(2)}) collective-permute-start(s32[6]{0:T(128)S(1)} %copy-done.3), channel_id=1, source_target_pairs={{0,32},{32,0},{1,33},{33,1},{2,34},{34,2},{3,35},{35,3},{4,36},{36... | collective-permute-start | bytes 80 | tf_op jit(solution)/shard_map/ppermute | solution.py:240
  89.5 0.8 collective-permute-done.5.other_ref
  90.3 1.0 shard_map.68
  91.3 4.1 %collective-permute-start.6 = (bf16[6,64,128]{2,1,0:T(8,128)(2,1)S(1)}, bf16[6,64,128]{2,1,0:T(8,128)(2,1)S(1)}, u32[]{:S(2)}, u32[]{:S(2)}) collective-permute-start(bf16[6,64,128]{2,1,0:T(8,128)(2,1)S(1)} %get-tuple-element.23), channel_id=1, source_target_pairs={{0,32},{32,0},{1,33},{33,1},{2,34},{34,2},{3,35},{35,3},{4,36},{36... | collective-permute-start | bytes 294920 | tf_op jit(solution)/shard_map/ppermute | solution.py:240
  95.4 6.8 %collective-permute-done.9.r3_ref = bf16[768,256]{1,0:T(8,128)(2,1)S(1)} collective-permute-done((bf16[768,256]{1,0:T(8,128)(2,1)S(1)}, bf16[768,256]{1,0:T(8,128)(2,1)S(1)}, u32[]{:S(2)}, u32[]{:S(2)}) %collective-permute-start.9) | collective-permute-done | bytes 393248 | tf_op jit(solution)/shard_map/ppermute | solution.py:240
  102.2 1.4 %shard_map.69 = bf16[768,256]{1,0:T(8,128)(2,1)} custom-call(s32[1]{0:T(128)} %bitcast.core_ref, bf16[32,80,128]{2,1,0:T(8,128)(2,1)S(1)} %all-to-all-done.2.pages_ref.low_ref, bf16[6,64,128]{2,1,0:T(8,128)(2,1)S(1)} %get-tuple-element.22.mine_ref, bf16[6,64,128]{2,1,0:T(8,128)(2,1)S(1)} %collective-permute-done.6.other_ref, f32[768,256]{1,0:T(8,128)S(1)} %copy-done.1, ...), custom_call_target="tpu_custom_call" | custom-call | flops 25165824 | bytes 3145728 | tf_op jit(solution)/shard_map/pallas_call | solution.py:221
  (31 shorter events, 0.9 us)
Async XLA Ops:
  0.0 12.0 %copy-start.6 = (bf16[4096,256]{1,0:T(8,128)(2,1)S(1)}, bf16[4096,256]{1,0:T(8,128)(2,1)}, u32[]{:S(2)}) copy-start(bf16[4096,256]{1,0:T(8,128)(2,1)} %refs_6_.1) | copy-start | bytes 6291460
  2.1 20.7 %copy-start.2 = (bf16[768,128]{1,0:T(8,128)(2,1)S(1)}, bf16[768,128]{1,0:T(8,128)(2,1)}, u32[]{:S(2)}) copy-start(bf16[768,128]{1,0:T(8,128)(2,1)} %attn_ref.1) | copy-start | bytes 589828
  2.1 38.7 %all-to-all-start = ((bf16[32,64,128]{2,1,0:T(8,128)(2,1)}), bf16[32,64,128]{2,1,0:T(8,128)(2,1)S(1)}, u32[]{:S(2)}, u32[]{:S(2)}) async-start(bf16[32,64,128]{2,1,0:T(8,128)(2,1)} %shard_map.64), calls=%async_computation | async-start | bytes 1048576 | tf_op jit(solution)/shard_map/all_to_all | solution.py:247
  12.0 34.2 %copy-start.3 = (s32[6]{0:T(128)S(1)}, s32[6]{0:T(128)}, u32[]{:S(2)}) copy-start(s32[6]{0:T(128)} %index_ref.2) | copy-start | bytes 76
  12.0 34.2 %copy-start.4 = (s32[32]{0:T(128)S(1)}, s32[32]{0:T(128)}, u32[]{:S(2)}) copy-start(s32[32]{0:T(128)} %table_ref.3) | copy-start | bytes 388
  13.2 41.2 %collective-permute-start.4 = (bf16[8,128,256]{2,1,0:T(8,128)(2,1)}, bf16[8,128,256]{2,1,0:T(8,128)(2,1)S(1)}, u32[]{:S(2)}, u32[]{:S(2)}) collective-permute-start(bf16[8,128,256]{2,1,0:T(8,128)(2,1)} %get-tuple-element.25), channel_id=1, source_target_pairs={{0,1},{1,2},{2,3},{3,0},{4,5},{5,6},{6,7},{7,4},{8,9},{9,10},{10,1... | collective-permute-start | bytes 1572872 | tf_op jit(solution)/shard_map/ppermute | solution.py:240
  16.3 38.1 %collective-permute-start.3 = (bf16[8,128,256]{2,1,0:T(8,128)(2,1)}, bf16[8,128,256]{2,1,0:T(8,128)(2,1)}, u32[]{:S(2)}, u32[]{:S(2)}) collective-permute-start(bf16[8,128,256]{2,1,0:T(8,128)(2,1)} %get-tuple-element.26), channel_id=1, source_target_pairs={{0,2},{1,3},{2,0},{3,1},{4,6},{5,7},{6,4},{7,5},{8,10},{9,11},{10,... | collective-permute-start | bytes 1572872 | tf_op jit(solution)/shard_map/ppermute | solution.py:240
  19.0 35.3 %collective-permute-start.2 = (bf16[8,128,256]{2,1,0:T(8,128)(2,1)S(1)}, bf16[8,128,256]{2,1,0:T(8,128)(2,1)}, u32[]{:S(2)}, u32[]{:S(2)}) collective-permute-start(bf16[8,128,256]{2,1,0:T(8,128)(2,1)S(1)} %get-tuple-element.27), channel_id=1, source_target_pairs={{0,3},{1,0},{2,1},{3,2},{4,7},{5,4},{6,5},{7,6},{8,11},{9,8},{10,9... | collective-permute-start | bytes 1572872 | tf_op jit(solution)/shard_map/ppermute | solution.py:240
  40.8 14.4 %copy-start.5 = (bf16[3072,128]{1,0:T(8,128)(2,1)}, bf16[3072,128]{1,0:T(8,128)(2,1)S(1)}, u32[]{:S(2)}) copy-start(bf16[3072,128]{1,0:T(8,128)(2,1)S(1)} %all-gather) | copy-start | bytes 2359300
  40.8 13.6 %collective-permute-start.1 = (bf16[2,768,128]{2,1,0:T(8,128)(2,1)S(1)}, bf16[2,768,128]{2,1,0:T(8,128)(2,1)}, u32[]{:S(2)}, u32[]{:S(2)}) collective-permute-start(bf16[2,768,128]{2,1,0:T(8,128)(2,1)S(1)} %get-tuple-element.28), channel_id=1, source_target_pairs={{0,28},{4,0},{8,4},{12,8},{16,12},{20,16},{24,20},{28,24},{1,29},{... | collective-permute-start | bytes 1179656 | tf_op jit(solution)/shard_map/ppermute | solution.py:240
  44.3 10.1 %collective-permute-start = (bf16[2,768,128]{2,1,0:T(8,128)(2,1)S(1)}, bf16[2,768,128]{2,1,0:T(8,128)(2,1)}, u32[]{:S(2)}, u32[]{:S(2)}) collective-permute-start(bf16[2,768,128]{2,1,0:T(8,128)(2,1)S(1)} %get-tuple-element.29), channel_id=1, source_target_pairs={{0,4},{4,8},{8,12},{12,16},{16,20},{20,24},{24,28},{28,0},{1,5},{5... | collective-permute-start | bytes 1179656 | tf_op jit(solution)/shard_map/ppermute | solution.py:240
  47.7 14.7 %all-to-all-start.1 = ((bf16[32,16,128]{2,1,0:T(8,128)(2,1)}), bf16[32,16,128]{2,1,0:T(8,128)(2,1)S(1)}, u32[]{:S(2)}, u32[]{:S(2)}) async-start(bf16[32,16,128]{2,1,0:T(8,128)(2,1)} %shard_map.65), calls=%async_computation.1 | async-start | bytes 262144 | tf_op jit(solution)/shard_map/all_to_all | solution.py:268
  54.3 0.8 copy-start.7
  55.1 7.3 %copy-start = (bf16[1,64,8192]{2,1,0:T(8,128)(2,1)S(1)}, bf16[1,64,8192]{2,1,0:T(8,128)(2,1)}, u32[]{:S(2)}) copy-start(bf16[1,64,8192]{2,1,0:T(8,128)(2,1)} %up_ref.1) | copy-start | bytes 3145732
  61.3 13.4 %copy-start.9 = (bf16[768,256]{1,0:T(8,128)(2,1)S(1)}, bf16[768,256]{1,0:T(8,128)(2,1)}, u32[]{:S(2)}) copy-start(bf16[768,256]{1,0:T(8,128)(2,1)} %get-tuple-element.18) | copy-start | bytes 1179652
  61.3 16.2 %copy-start.8 = (bf16[768,256]{1,0:T(8,128)(2,1)S(1)}, bf16[768,256]{1,0:T(8,128)(2,1)}, u32[]{:S(2)}) copy-start(bf16[768,256]{1,0:T(8,128)(2,1)} %get-tuple-element.19) | copy-start | bytes 1179652
  61.3 40.8 %copy-start.1 = (f32[768,256]{1,0:T(8,128)S(1)}, f32[768,256]{1,0:T(8,128)}, u32[]{:S(2)}) copy-start(f32[768,256]{1,0:T(8,128)} %get-tuple-element.24.own_hbm) | copy-start | bytes 2359300
  63.5 26.9 %all-to-all-start.2 = ((bf16[32,80,128]{2,1,0:T(8,128)(2,1)}), bf16[32,80,128]{2,1,0:T(8,128)(2,1)S(1)}, u32[]{:S(2)}, u32[]{:S(2)}) async-start(bf16[32,80,128]{2,1,0:T(8,128)(2,1)} %shard_map.67), calls=%async_computation.2 | async-start | bytes 1310720 | tf_op jit(solution)/shard_map/all_to_all | solution.py:275
  71.6 23.8 %collective-permute-start.7 = (bf16[768,256]{1,0:T(8,128)(2,1)}, bf16[768,256]{1,0:T(8,128)(2,1)S(1)}, u32[]{:S(2)}, u32[]{:S(2)}) collective-permute-start(bf16[768,256]{1,0:T(8,128)(2,1)} %get-tuple-element.17), channel_id=1, source_target_pairs={{0,1},{1,2},{2,3},{3,0},{4,5},{5,6},{6,7},{7,4},{8,9},{9,10},{10,1... | collective-permute-start | bytes 1179656 | tf_op jit(solution)/shard_map/ppermute | solution.py:240
  74.7 20.7 %collective-permute-start.8 = (bf16[768,256]{1,0:T(8,128)(2,1)S(1)}, bf16[768,256]{1,0:T(8,128)(2,1)S(1)}, u32[]{:S(2)}, u32[]{:S(2)}) collective-permute-start(bf16[768,256]{1,0:T(8,128)(2,1)S(1)} %copy-done.9), channel_id=1, source_target_pairs={{0,2},{1,3},{2,0},{3,1},{4,6},{5,7},{6,4},{7,5},{8,10},{9,11},{10,... | collective-permute-start | bytes 1179656 | tf_op jit(solution)/shard_map/ppermute | solution.py:240
  77.5 24.7 %collective-permute-start.9 = (bf16[768,256]{1,0:T(8,128)(2,1)S(1)}, bf16[768,256]{1,0:T(8,128)(2,1)S(1)}, u32[]{:S(2)}, u32[]{:S(2)}) collective-permute-start(bf16[768,256]{1,0:T(8,128)(2,1)S(1)} %copy-done.8), channel_id=1, source_target_pairs={{0,3},{1,0},{2,1},{3,2},{4,7},{5,4},{6,5},{7,6},{8,11},{9,8},{10,9... | collective-permute-start | bytes 1179656 | tf_op jit(solution)/shard_map/ppermute | solution.py:240
  81.2 9.1 %collective-permute-start.5 = (s32[6]{0:T(128)S(1)}, s32[6]{0:T(128)S(1)}, u32[]{:S(2)}, u32[]{:S(2)}) collective-permute-start(s32[6]{0:T(128)S(1)} %copy-done.3), channel_id=1, source_target_pairs={{0,32},{32,0},{1,33},{33,1},{2,34},{34,2},{3,35},{35,3},{4,36},{36... | collective-permute-start | bytes 80 | tf_op jit(solution)/shard_map/ppermute | solution.py:240
  91.3 10.8 %collective-permute-start.6 = (bf16[6,64,128]{2,1,0:T(8,128)(2,1)S(1)}, bf16[6,64,128]{2,1,0:T(8,128)(2,1)S(1)}, u32[]{:S(2)}, u32[]{:S(2)}) collective-permute-start(bf16[6,64,128]{2,1,0:T(8,128)(2,1)S(1)} %get-tuple-element.23), channel_id=1, source_target_pairs={{0,32},{32,0},{1,33},{33,1},{2,34},{34,2},{3,35},{35,3},{4,36},{36... | collective-permute-start | bytes 294920 | tf_op jit(solution)/shard_map/ppermute | solution.py:240

commit v3 on v2

--- a/solution.py
+++ b/solution.py
@@ -134,7 +134,9 @@
 def product_kernel(n, parts, parity_ref, x_ref, *refs):
     offsets = [o for p in parts for o in p]
     xs, weights, outs = refs[: len(parts)], refs[len(parts) : len(parts) + n], refs[len(parts) + n : len(parts) + 2 * n]
-    gathered, held, x_sems, w_sems = refs[len(parts) + 2 * n :]
+    gathered, held, x_sems, w_sems = refs[len(parts) + 2 * n : len(parts) + 2 * n + 4]
+    made, o_sems = refs[len(parts) + 2 * n + 4 : -1], refs[-1]
+    leaving = [pltpu.make_async_copy(made[k], outs[k], o_sems.at[k]) for k in range(n)]
     parity = parity_ref[0]
     ny, own = held.shape[1], held.shape[2]
     at, copies = 0, []
@@ -163,7 +165,10 @@
         for m in range(0, gathered.shape[1], 256):
             rows = slice(m, m + 256)
             x = jnp.concatenate([gathered[j, rows, :] for j in range(ny)], axis=1)
-            outs[k][rows, :] = jnp.dot(x, w, preferred_element_type=jnp.float32).astype(outs[k].dtype)
+            made[k][rows, :] = jnp.dot(x, w, preferred_element_type=jnp.float32).astype(outs[k].dtype)
+        leaving[k].start()
+    for c in leaving:
+        c.wait()
 
 
 def product(scalars, gathered, parts, weights, dtypes):
@@ -175,12 +180,14 @@
         functools.partial(product_kernel, n, parts),
         out_shape=[jax.ShapeDtypeStruct((tokens, width), d) for d in dtypes],
         in_specs=[SMEM] * 2 + [ANY] * (len(gathered) + n),
-        out_specs=[VMEM] * n,
+        out_specs=[ANY] * n,
         scratch_shapes=[
             pltpu.VMEM((ny, tokens, own), gathered[0].dtype),
             pltpu.VMEM((n, ny, own, width), weights[0].dtype),
             pltpu.SemaphoreType.DMA((len(gathered),)),
             pltpu.SemaphoreType.DMA((n, ny)),
+            *(pltpu.VMEM((tokens, width), d) for d in dtypes),
+            pltpu.SemaphoreType.DMA((n,)),
         ],
         compiler_params=params(WHOLE),
         cost_estimate=cost(2 * n * MIB, 2 * tokens * ny * own * width * n),

time: 104 us -> 104 us (level)
  the two profiles are of different devices: /device:TPU:387 before, /device:TPU:131 now
where the time goes in v3:
time: 104 us
  starting transfers between devices  61.5 us (59%)
  blocking collectives  18 us (17%)
  Pallas kernels  13.1 us (13%)
  waiting for transfers between devices  8.66 us (8%)
  local copies, waits for them, and re-layouts  1.98 us (2%)
    ppermute x10, starting transfers between devices, shift(): return lax.ppermute(a, axis, [(i, (i + by) % size) for i in range(size)])  36.9 us
    all_gather x1, blocking collectives, local(): same = lax.all_gather(attn, 'yh')  18 us
    all_to_all x1, starting transfers between devices, local(): pages = lax.all_to_all(pack(down, tp), tps, 0, 0, tiled=True)  9.83 us
    all_to_all x1, starting transfers between devices, local(): low = lax.all_to_all(summed, tps, 0, 0, tiled=True)  8.17 us
    ppermute x10, waiting for transfers between devices, shift(): return lax.ppermute(a, axis, [(i, (i + by) % size) for i in range(size)])  7.58 us
    all_to_all x1, starting transfers between devices, local(): pieces = lax.all_to_all(pieces, tps, 0, 0, tiled=True)  6.6 us
    pallas_call x1, Pallas kernels, product(): pl.pallas_call(functools.partial(product_kernel, n, parts), out_shape=[ja...  6.19 us
    pallas_call x1, Pallas kernels, pack(): pl.pallas_call(pack_kernel, out_shape=jax.ShapeDtypeStruct((tp, RANK, dow...  2.09 us
  transfers between devices with their start and end apart: 13, of which 3 were waited for; matrix products, arithmetic and copies ran while one was open for 1% of the time, Pallas kernels for 8%

profile of v3, /device:TPU:131, one launch (start us, length us, event | category | flops | bytes accessed | tf_op | source)
XLA Modules:
  0.0 103.6 jit_solution(16043576752786794534)
XLA Ops:
  0.0 2.1 %shard_map.64 = bf16[32,64,128]{2,1,0:T(8,128)(2,1)} custom-call(bf16[1,64,4096]{2,1,0:T(8,128)(2,1)} %down_ref.1), custom_call_target="tpu_custom_call" | custom-call | bytes 1048576 | tf_op jit(solution)/shard_map/pallas_call | solution.py:42
  2.1 9.8 %all-to-all-start = ((bf16[32,64,128]{2,1,0:T(8,128)(2,1)}), bf16[32,64,128]{2,1,0:T(8,128)(2,1)S(1)}, u32[]{:S(2)}, u32[]{:S(2)}) async-start(bf16[32,64,128]{2,1,0:T(8,128)(2,1)} %shard_map.64), calls=%async_computation | async-start | bytes 1048576 | tf_op jit(solution)/shard_map/all_to_all | solution.py:254
  12.0 1.1 %dynamic-slice_bitcast_fusion = (bf16[8,128,256]{2,1,0:T(8,128)(2,1)}, bf16[8,128,256]{2,1,0:T(8,128)(2,1)}, bf16[8,128,256]{2,1,0:T(8,128)(2,1)S(1)}) fusion(bf16[8,4,128,256]{3,2,1,0:T(8,128)(2,1)S(1)} %bitcast.19, s32[]{:T(128)S(6)} %select_n.30, s32[]{:T(128)S(6)} %select_n.28, s32[]{:T(128)S(6)} %select_n.26), kind=kLoop, calls=%fused_computation | loop fusion | bytes 3145740 | tf_op jit(solution)/shard_map/jit(dynamic_index_in_dim)/squeeze | solution.py:269
  13.2 3.1 %collective-permute-start.4 = (bf16[8,128,256]{2,1,0:T(8,128)(2,1)}, bf16[8,128,256]{2,1,0:T(8,128)(2,1)S(1)}, u32[]{:S(2)}, u32[]{:S(2)}) collective-permute-start(bf16[8,128,256]{2,1,0:T(8,128)(2,1)} %get-tuple-element.25), channel_id=1, source_target_pairs={{0,1},{1,2},{2,3},{3,0},{4,5},{5,6},{6,7},{7,4},{8,9},{9,10},{10,1... | collective-permute-start | bytes 1572872 | tf_op jit(solution)/shard_map/ppermute | solution.py:247
  16.3 2.8 %collective-permute-start.3 = (bf16[8,128,256]{2,1,0:T(8,128)(2,1)}, bf16[8,128,256]{2,1,0:T(8,128)(2,1)}, u32[]{:S(2)}, u32[]{:S(2)}) collective-permute-start(bf16[8,128,256]{2,1,0:T(8,128)(2,1)} %get-tuple-element.26), channel_id=1, source_target_pairs={{0,2},{1,3},{2,0},{3,1},{4,6},{5,7},{6,4},{7,5},{8,10},{9,11},{10,... | collective-permute-start | bytes 1572872 | tf_op jit(solution)/shard_map/ppermute | solution.py:247
  19.0 3.7 %collective-permute-start.2 = (bf16[8,128,256]{2,1,0:T(8,128)(2,1)S(1)}, bf16[8,128,256]{2,1,0:T(8,128)(2,1)}, u32[]{:S(2)}, u32[]{:S(2)}) collective-permute-start(bf16[8,128,256]{2,1,0:T(8,128)(2,1)S(1)} %get-tuple-element.27), channel_id=1, source_target_pairs={{0,3},{1,0},{2,1},{3,2},{4,7},{5,4},{6,5},{7,6},{8,11},{9,8},{10,9... | collective-permute-start | bytes 1572872 | tf_op jit(solution)/shard_map/ppermute | solution.py:247
  22.8 18.0 %all-gather = bf16[3072,128]{1,0:T(8,128)(2,1)S(1)} all-gather(bf16[768,128]{1,0:T(8,128)(2,1)S(1)} %copy-done.2), channel_id=2, replica_groups=mesh['z'=8,'core'=2,'yh'=4,'yl'=2,'x'=4] {'yh'}, dimensions={0}, use_global_device_ids=true | all-gather | bytes 983040 | tf_op jit(solution)/shard_map/all_gather | solution.py:256
  40.8 3.5 %collective-permute-start.1 = (bf16[2,768,128]{2,1,0:T(8,128)(2,1)S(1)}, bf16[2,768,128]{2,1,0:T(8,128)(2,1)}, u32[]{:S(2)}, u32[]{:S(2)}) collective-permute-start(bf16[2,768,128]{2,1,0:T(8,128)(2,1)S(1)} %get-tuple-element.28), channel_id=1, source_target_pairs={{0,28},{4,0},{8,4},{12,8},{16,12},{20,16},{24,20},{28,24},{1,29},{... | collective-permute-start | bytes 1179656 | tf_op jit(solution)/shard_map/ppermute | solution.py:247
  44.3 1.9 %collective-permute-start = (bf16[2,768,128]{2,1,0:T(8,128)(2,1)S(1)}, bf16[2,768,128]{2,1,0:T(8,128)(2,1)}, u32[]{:S(2)}, u32[]{:S(2)}) collective-permute-start(bf16[2,768,128]{2,1,0:T(8,128)(2,1)S(1)} %get-tuple-element.29), channel_id=1, source_target_pairs={{0,4},{4,8},{8,12},{12,16},{16,20},{20,24},{24,28},{28,0},{1,5},{5... | collective-permute-start | bytes 1179656 | tf_op jit(solution)/shard_map/ppermute | solution.py:247
  46.3 1.5 %shard_map.65 = bf16[32,16,128]{2,1,0:T(8,128)(2,1)} custom-call(s32[6]{0:T(128)S(1)} %copy-done.3, s32[32]{0:T(128)S(1)} %copy-done.4, bf16[768,128]{1,0:T(8,128)(2,1)S(1)} %copy-done.2, bf16[32,64,128]{2,1,0:T(8,128)(2,1)S(1)} %all-to-all-done.pages_ref), custom_call_target="tpu_custom_call" | custom-call | flops 12582912 | bytes 524288 | tf_op jit(solution)/shard_map/pallas_call | solution.py:70
  47.7 6.6 %all-to-all-start.1 = ((bf16[32,16,128]{2,1,0:T(8,128)(2,1)}), bf16[32,16,128]{2,1,0:T(8,128)(2,1)S(1)}, u32[]{:S(2)}, u32[]{:S(2)}) async-start(bf16[32,16,128]{2,1,0:T(8,128)(2,1)} %shard_map.65), calls=%async_computation.1 | async-start | bytes 262144 | tf_op jit(solution)/shard_map/all_to_all | solution.py:275
  55.1 6.2 %shard_map.66 = (bf16[768,256]{1,0:T(8,128)(2,1)}, bf16[768,256]{1,0:T(8,128)(2,1)}, bf16[768,256]{1,0:T(8,128)(2,1)}, f32[768,256]{1,0:T(8,128)}) custom-call(s32[1]{0:T(128)} %bitcast.2.parity_ref, s32[1]{0:T(128)} %bitcast.3.x_ref, bf16[4,768,128]{2,1,0:T(8,128)(2,1)} %bitcast.18, bf16[2,768,128]{2,1,0:T(8,128)(2,1)} %collective-permute-done.refs_1_, ...), custom_call_target="tpu_custom_call" | custom-call | flops 1610612736 | bytes 8388608 | tf_op jit(solution)/shard_map/pallas_call | solution.py:179
  61.4 1.1 %all-to-all-done.1.in_ref = bf16[32,16,128]{2,1,0:T(8,128)(2,1)S(1)} async-done(((bf16[32,16,128]{2,1,0:T(8,128)(2,1)}), bf16[32,16,128]{2,1,0:T(8,128)(2,1)S(1)}, u32[]{:S(2)}, u32[]{:S(2)}) %all-to-all-start.1) | async-done | bytes 131104 | tf_op jit(solution)/shard_map/all_to_all | solution.py:275
  62.5 1.0 shard_map.67
  63.5 8.2 %all-to-all-start.2 = ((bf16[32,80,128]{2,1,0:T(8,128)(2,1)}), bf16[32,80,128]{2,1,0:T(8,128)(2,1)S(1)}, u32[]{:S(2)}, u32[]{:S(2)}) async-start(bf16[32,80,128]{2,1,0:T(8,128)(2,1)} %shard_map.67), calls=%async_computation.2 | async-start | bytes 1310720 | tf_op jit(solution)/shard_map/all_to_all | solution.py:282
  71.6 3.1 %collective-permute-start.7 = (bf16[768,256]{1,0:T(8,128)(2,1)}, bf16[768,256]{1,0:T(8,128)(2,1)S(1)}, u32[]{:S(2)}, u32[]{:S(2)}) collective-permute-start(bf16[768,256]{1,0:T(8,128)(2,1)} %get-tuple-element.17), channel_id=1, source_target_pairs={{0,1},{1,2},{2,3},{3,0},{4,5},{5,6},{6,7},{7,4},{8,9},{9,10},{10,1... | collective-permute-start | bytes 1179656 | tf_op jit(solution)/shard_map/ppermute | solution.py:247
  74.8 2.7 %collective-permute-start.8 = (bf16[768,256]{1,0:T(8,128)(2,1)S(1)}, bf16[768,256]{1,0:T(8,128)(2,1)S(1)}, u32[]{:S(2)}, u32[]{:S(2)}) collective-permute-start(bf16[768,256]{1,0:T(8,128)(2,1)S(1)} %copy-done.9), channel_id=1, source_target_pairs={{0,2},{1,3},{2,0},{3,1},{4,6},{5,7},{6,4},{7,5},{8,10},{9,11},{10,... | collective-permute-start | bytes 1179656 | tf_op jit(solution)/shard_map/ppermute | solution.py:247
  77.5 3.7 %collective-permute-start.9 = (bf16[768,256]{1,0:T(8,128)(2,1)S(1)}, bf16[768,256]{1,0:T(8,128)(2,1)S(1)}, u32[]{:S(2)}, u32[]{:S(2)}) collective-permute-start(bf16[768,256]{1,0:T(8,128)(2,1)S(1)} %copy-done.8), channel_id=1, source_target_pairs={{0,3},{1,0},{2,1},{3,2},{4,7},{5,4},{6,5},{7,6},{8,11},{9,8},{10,9... | collective-permute-start | bytes 1179656 | tf_op jit(solution)/shard_map/ppermute | solution.py:247
  81.3 8.3 %collective-permute-start.5 = (s32[6]{0:T(128)S(1)}, s32[6]{0:T(128)S(1)}, u32[]{:S(2)}, u32[]{:S(2)}) collective-permute-start(s32[6]{0:T(128)S(1)} %copy-done.3), channel_id=1, source_target_pairs={{0,32},{32,0},{1,33},{33,1},{2,34},{34,2},{3,35},{35,3},{4,36},{36... | collective-permute-start | bytes 80 | tf_op jit(solution)/shard_map/ppermute | solution.py:247
  89.6 0.8 collective-permute-done.5.other_ref
  90.4 1.0 shard_map.68
  91.3 4.1 %collective-permute-start.6 = (bf16[6,64,128]{2,1,0:T(8,128)(2,1)S(1)}, bf16[6,64,128]{2,1,0:T(8,128)(2,1)S(1)}, u32[]{:S(2)}, u32[]{:S(2)}) collective-permute-start(bf16[6,64,128]{2,1,0:T(8,128)(2,1)S(1)} %get-tuple-element.23), channel_id=1, source_target_pairs={{0,32},{32,0},{1,33},{33,1},{2,34},{34,2},{3,35},{35,3},{4,36},{36... | collective-permute-start | bytes 294920 | tf_op jit(solution)/shard_map/ppermute | solution.py:247
  95.4 6.8 %collective-permute-done.9.r3_ref = bf16[768,256]{1,0:T(8,128)(2,1)S(1)} collective-permute-done((bf16[768,256]{1,0:T(8,128)(2,1)S(1)}, bf16[768,256]{1,0:T(8,128)(2,1)S(1)}, u32[]{:S(2)}, u32[]{:S(2)}) %collective-permute-start.9) | collective-permute-done | bytes 393248 | tf_op jit(solution)/shard_map/ppermute | solution.py:247
  102.2 1.4 %shard_map.69 = bf16[768,256]{1,0:T(8,128)(2,1)} custom-call(s32[1]{0:T(128)} %bitcast.core_ref, bf16[32,80,128]{2,1,0:T(8,128)(2,1)S(1)} %all-to-all-done.2.pages_ref.low_ref, bf16[6,64,128]{2,1,0:T(8,128)(2,1)S(1)} %get-tuple-element.22.mine_ref, bf16[6,64,128]{2,1,0:T(8,128)(2,1)S(1)} %collective-permute-done.6.other_ref, f32[768,256]{1,0:T(8,128)S(1)} %copy-done.1, ...), custom_call_target="tpu_custom_call" | custom-call | flops 25165824 | bytes 3145728 | tf_op jit(solution)/shard_map/pallas_call | solution.py:228
  (31 shorter events, 0.9 us)
Async XLA Ops:
  0.0 12.0 %copy-start.6 = (bf16[4096,256]{1,0:T(8,128)(2,1)S(1)}, bf16[4096,256]{1,0:T(8,128)(2,1)}, u32[]{:S(2)}) copy-start(bf16[4096,256]{1,0:T(8,128)(2,1)} %refs_6_.1) | copy-start | bytes 6291460
  2.1 20.7 %copy-start.2 = (bf16[768,128]{1,0:T(8,128)(2,1)S(1)}, bf16[768,128]{1,0:T(8,128)(2,1)}, u32[]{:S(2)}) copy-start(bf16[768,128]{1,0:T(8,128)(2,1)} %attn_ref.1) | copy-start | bytes 589828
  2.1 38.7 %all-to-all-start = ((bf16[32,64,128]{2,1,0:T(8,128)(2,1)}), bf16[32,64,128]{2,1,0:T(8,128)(2,1)S(1)}, u32[]{:S(2)}, u32[]{:S(2)}) async-start(bf16[32,64,128]{2,1,0:T(8,128)(2,1)} %shard_map.64), calls=%async_computation | async-start | bytes 1048576 | tf_op jit(solution)/shard_map/all_to_all | solution.py:254
  12.0 34.2 %copy-start.3 = (s32[6]{0:T(128)S(1)}, s32[6]{0:T(128)}, u32[]{:S(2)}) copy-start(s32[6]{0:T(128)} %index_ref.2) | copy-start | bytes 76
  12.0 34.2 %copy-start.4 = (s32[32]{0:T(128)S(1)}, s32[32]{0:T(128)}, u32[]{:S(2)}) copy-start(s32[32]{0:T(128)} %table_ref.3) | copy-start | bytes 388
  13.2 41.2 %collective-permute-start.4 = (bf16[8,128,256]{2,1,0:T(8,128)(2,1)}, bf16[8,128,256]{2,1,0:T(8,128)(2,1)S(1)}, u32[]{:S(2)}, u32[]{:S(2)}) collective-permute-start(bf16[8,128,256]{2,1,0:T(8,128)(2,1)} %get-tuple-element.25), channel_id=1, source_target_pairs={{0,1},{1,2},{2,3},{3,0},{4,5},{5,6},{6,7},{7,4},{8,9},{9,10},{10,1... | collective-permute-start | bytes 1572872 | tf_op jit(solution)/shard_map/ppermute | solution.py:247
  16.3 38.1 %collective-permute-start.3 = (bf16[8,128,256]{2,1,0:T(8,128)(2,1)}, bf16[8,128,256]{2,1,0:T(8,128)(2,1)}, u32[]{:S(2)}, u32[]{:S(2)}) collective-permute-start(bf16[8,128,256]{2,1,0:T(8,128)(2,1)} %get-tuple-element.26), channel_id=1, source_target_pairs={{0,2},{1,3},{2,0},{3,1},{4,6},{5,7},{6,4},{7,5},{8,10},{9,11},{10,... | collective-permute-start | bytes 1572872 | tf_op jit(solution)/shard_map/ppermute | solution.py:247
  19.0 35.3 %collective-permute-start.2 = (bf16[8,128,256]{2,1,0:T(8,128)(2,1)S(1)}, bf16[8,128,256]{2,1,0:T(8,128)(2,1)}, u32[]{:S(2)}, u32[]{:S(2)}) collective-permute-start(bf16[8,128,256]{2,1,0:T(8,128)(2,1)S(1)} %get-tuple-element.27), channel_id=1, source_target_pairs={{0,3},{1,0},{2,1},{3,2},{4,7},{5,4},{6,5},{7,6},{8,11},{9,8},{10,9... | collective-permute-start | bytes 1572872 | tf_op jit(solution)/shard_map/ppermute | solution.py:247
  40.8 14.4 %copy-start.5 = (bf16[3072,128]{1,0:T(8,128)(2,1)}, bf16[3072,128]{1,0:T(8,128)(2,1)S(1)}, u32[]{:S(2)}) copy-start(bf16[3072,128]{1,0:T(8,128)(2,1)S(1)} %all-gather) | copy-start | bytes 2359300
  40.8 13.6 %collective-permute-start.1 = (bf16[2,768,128]{2,1,0:T(8,128)(2,1)S(1)}, bf16[2,768,128]{2,1,0:T(8,128)(2,1)}, u32[]{:S(2)}, u32[]{:S(2)}) collective-permute-start(bf16[2,768,128]{2,1,0:T(8,128)(2,1)S(1)} %get-tuple-element.28), channel_id=1, source_target_pairs={{0,28},{4,0},{8,4},{12,8},{16,12},{20,16},{24,20},{28,24},{1,29},{... | collective-permute-start | bytes 1179656 | tf_op jit(solution)/shard_map/ppermute | solution.py:247
  44.3 10.1 %collective-permute-start = (bf16[2,768,128]{2,1,0:T(8,128)(2,1)S(1)}, bf16[2,768,128]{2,1,0:T(8,128)(2,1)}, u32[]{:S(2)}, u32[]{:S(2)}) collective-permute-start(bf16[2,768,128]{2,1,0:T(8,128)(2,1)S(1)} %get-tuple-element.29), channel_id=1, source_target_pairs={{0,4},{4,8},{8,12},{12,16},{16,20},{20,24},{24,28},{28,0},{1,5},{5... | collective-permute-start | bytes 1179656 | tf_op jit(solution)/shard_map/ppermute | solution.py:247
  47.7 14.7 %all-to-all-start.1 = ((bf16[32,16,128]{2,1,0:T(8,128)(2,1)}), bf16[32,16,128]{2,1,0:T(8,128)(2,1)S(1)}, u32[]{:S(2)}, u32[]{:S(2)}) async-start(bf16[32,16,128]{2,1,0:T(8,128)(2,1)} %shard_map.65), calls=%async_computation.1 | async-start | bytes 262144 | tf_op jit(solution)/shard_map/all_to_all | solution.py:275
  54.3 0.8 copy-start.7
  55.1 7.3 %copy-start = (bf16[1,64,8192]{2,1,0:T(8,128)(2,1)S(1)}, bf16[1,64,8192]{2,1,0:T(8,128)(2,1)}, u32[]{:S(2)}) copy-start(bf16[1,64,8192]{2,1,0:T(8,128)(2,1)} %up_ref.1) | copy-start | bytes 3145732
  61.3 13.4 %copy-start.9 = (bf16[768,256]{1,0:T(8,128)(2,1)S(1)}, bf16[768,256]{1,0:T(8,128)(2,1)}, u32[]{:S(2)}) copy-start(bf16[768,256]{1,0:T(8,128)(2,1)} %get-tuple-element.18) | copy-start | bytes 1179652
  61.4 16.2 %copy-start.8 = (bf16[768,256]{1,0:T(8,128)(2,1)S(1)}, bf16[768,256]{1,0:T(8,128)(2,1)}, u32[]{:S(2)}) copy-start(bf16[768,256]{1,0:T(8,128)(2,1)} %get-tuple-element.19) | copy-start | bytes 1179652
  61.4 40.8 %copy-start.1 = (f32[768,256]{1,0:T(8,128)S(1)}, f32[768,256]{1,0:T(8,128)}, u32[]{:S(2)}) copy-start(f32[768,256]{1,0:T(8,128)} %get-tuple-element.24.own_hbm) | copy-start | bytes 2359300
  63.5 26.9 %all-to-all-start.2 = ((bf16[32,80,128]{2,1,0:T(8,128)(2,1)}), bf16[32,80,128]{2,1,0:T(8,128)(2,1)S(1)}, u32[]{:S(2)}, u32[]{:S(2)}) async-start(bf16[32,80,128]{2,1,0:T(8,128)(2,1)} %shard_map.67), calls=%async_computation.2 | async-start | bytes 1310720 | tf_op jit(solution)/shard_map/all_to_all | solution.py:282
  71.6 23.8 %collective-permute-start.7 = (bf16[768,256]{1,0:T(8,128)(2,1)}, bf16[768,256]{1,0:T(8,128)(2,1)S(1)}, u32[]{:S(2)}, u32[]{:S(2)}) collective-permute-start(bf16[768,256]{1,0:T(8,128)(2,1)} %get-tuple-element.17), channel_id=1, source_target_pairs={{0,1},{1,2},{2,3},{3,0},{4,5},{5,6},{6,7},{7,4},{8,9},{9,10},{10,1... | collective-permute-start | bytes 1179656 | tf_op jit(solution)/shard_map/ppermute | solution.py:247
  74.8 20.7 %collective-permute-start.8 = (bf16[768,256]{1,0:T(8,128)(2,1)S(1)}, bf16[768,256]{1,0:T(8,128)(2,1)S(1)}, u32[]{:S(2)}, u32[]{:S(2)}) collective-permute-start(bf16[768,256]{1,0:T(8,128)(2,1)S(1)} %copy-done.9), channel_id=1, source_target_pairs={{0,2},{1,3},{2,0},{3,1},{4,6},{5,7},{6,4},{7,5},{8,10},{9,11},{10,... | collective-permute-start | bytes 1179656 | tf_op jit(solution)/shard_map/ppermute | solution.py:247
  77.5 24.7 %collective-permute-start.9 = (bf16[768,256]{1,0:T(8,128)(2,1)S(1)}, bf16[768,256]{1,0:T(8,128)(2,1)S(1)}, u32[]{:S(2)}, u32[]{:S(2)}) collective-permute-start(bf16[768,256]{1,0:T(8,128)(2,1)S(1)} %copy-done.8), channel_id=1, source_target_pairs={{0,3},{1,0},{2,1},{3,2},{4,7},{5,4},{6,5},{7,6},{8,11},{9,8},{10,9... | collective-permute-start | bytes 1179656 | tf_op jit(solution)/shard_map/ppermute | solution.py:247
  81.3 9.1 %collective-permute-start.5 = (s32[6]{0:T(128)S(1)}, s32[6]{0:T(128)S(1)}, u32[]{:S(2)}, u32[]{:S(2)}) collective-permute-start(s32[6]{0:T(128)S(1)} %copy-done.3), channel_id=1, source_target_pairs={{0,32},{32,0},{1,33},{33,1},{2,34},{34,2},{3,35},{35,3},{4,36},{36... | collective-permute-start | bytes 80 | tf_op jit(solution)/shard_map/ppermute | solution.py:247
  91.3 10.8 %collective-permute-start.6 = (bf16[6,64,128]{2,1,0:T(8,128)(2,1)S(1)}, bf16[6,64,128]{2,1,0:T(8,128)(2,1)S(1)}, u32[]{:S(2)}, u32[]{:S(2)}) collective-permute-start(bf16[6,64,128]{2,1,0:T(8,128)(2,1)S(1)} %get-tuple-element.23), channel_id=1, source_target_pairs={{0,32},{32,0},{1,33},{33,1},{2,34},{34,2},{3,35},{35,3},{4,36},{36... | collective-permute-start | bytes 294920 | tf_op jit(solution)/shard_map/ppermute | solution.py:247
